TPU v7x, 32 devices: a whole 2x2x4 slice. The times are simulated.
32 devices in a mesh: row: 16 (over z, y, x), col: 2 (over core).
Axes of the slice: x: 2, y: 2, z: 4, core: 2. Of those that a mesh axis runs over, the one named last changes fastest.
Arguments:
- latent: bfloat16 [6144, 512], P('row', 'col'), may hold values from -6 to 6
- w_kv: bfloat16 [512, 8192], P('row', 'col'), may hold values from -0.25 to 0.25
- queries: bfloat16 [6144, 4096], P('row', 'col'), may hold values from -240 to 240
- w_out: bfloat16 [4096, 7168], P('row', 'col'), may hold values from -0.09375 to 0.09375
Outputs:
- mixed: bfloat16 [6144, 7168], P('row', 'col')
All inputs are finite; a program needn't handle non-finite values.
Results may differ from a plain program's by a relative error of at most 0.012.
The roundings to bfloat16 on the way count: a program that leaves them out, or rounds other values in their place, can miss the bound.
Values may be sent and summed in bfloat16 or wider, within the bound.
No kernel may reach another device: no remote copies, remote signals or barrier semaphores. Data moves between devices by JAX's collectives and lax.ppermute only.
A program may use at most 128 MiB of HBM per device.

v0:
```python
import functools
import math

import jax
import jax.numpy as jnp
from jax import lax
from jax.experimental import pallas as pl
from jax.experimental.pallas import tpu as pltpu
from jax.sharding import Mesh, PartitionSpec as P


HEAD = 128
NEG_FILL = -1e30
VMEM_LIMIT = 56 * 1024 * 1024


def cut_kernel(place, *refs, takes):
    ins, outs = refs[: len(takes)], refs[len(takes) :]
    mem = place[1]
    at = 0
    for ref, take in zip(ins, takes):
        for m, stride, parts in take:
            done = 0
            for offset, width in parts:
                first = pl.multiple_of((mem ^ m) * stride + offset, HEAD)
                outs[at][:, done : done + width] = ref[:, pl.ds(first, width)]
                done += width
            at += 1


def cut(place, arrays, takes):
    flat = [(x, take) for x, some in zip(arrays, takes) for take in some]
    widths = [n for _, (_, stride, parts) in flat for n in (stride, *(v for p in parts for v in p))]
    if any(n % HEAD for n in widths):
        mem = place[1]
        return [
            jnp.concatenate(
                [lax.dynamic_slice_in_dim(x, (mem ^ m) * stride + o, n, 1) for o, n in parts], axis=1
            )
            for x, (m, stride, parts) in flat
        ]
    return pl.pallas_call(
        functools.partial(cut_kernel, takes=takes),
        out_shape=[
            jax.ShapeDtypeStruct((x.shape[0], sum(n for _, n in parts)), x.dtype)
            for x, (_, _, parts) in flat
        ],
        grid_spec=pltpu.PrefetchScalarGridSpec(
            num_scalar_prefetch=1,
            grid=(1,),
            in_specs=[pl.BlockSpec(x.shape, lambda i, s: (0, 0)) for x in arrays],
            out_specs=[
                pl.BlockSpec((x.shape[0], sum(n for _, n in parts)), lambda i, s: (0, 0))
                for x, (_, _, parts) in flat
            ],
        ),
        compiler_params=pltpu.CompilerParams(vmem_limit_bytes=VMEM_LIMIT),
        cost_estimate=pl.CostEstimate(
            flops=0, transcendentals=0, bytes_accessed=2 * sum(2 * x.size for x in arrays)
        ),
        name="cut",
    )(place, *arrays)


def attention_kernel(place, *refs, planes, group, cols, rate, parts):
    q_refs, refs = refs[:group], refs[group:]
    own, refs = refs[: cols * group], refs[cols * group :]
    before, refs = refs[: cols * group], refs[cols * group :]
    w_refs, refs = refs[:planes], refs[planes:]
    o_ref, q_sc, w_sc, kv_sc, m_sc, acc_sc = refs
    grp, mem, col = place[0], place[1], place[2]
    tok, features = own[0].shape
    plane = tok * group
    earlier = (planes - 1) * plane
    block = pl.program_id(1)
    size = o_ref.shape[0]
    rows = size // parts
    depth = w_refs[0].shape[1]

    def expand(sources, at, to):
        out = None
        for s in range(cols):
            w = w_sc[pl.ds(pl.multiple_of(((col + s) % cols) * features, features), features), :]
            term = jnp.dot(sources[s * group][at, :], w, preferred_element_type=jnp.float32)
            out = term if out is None else out + term
        kv_sc[to, :] = out.astype(kv_sc.dtype)

    @pl.when(block == 0)
    def _():
        for m in range(group):
            q_sc[pl.ds(pl.multiple_of((mem ^ m) * tok, tok), tok), :] = q_refs[m][...]
            for k in range(planes):
                first = ((grp ^ k) * group + (mem ^ m)) * depth
                w_sc[pl.ds(pl.multiple_of(first, depth), depth), :] = w_refs[k][m]
        for m in range(group):
            first = earlier + (mem ^ m) * tok
            expand(own[m:], pl.ds(0, tok), pl.ds(pl.multiple_of(first, tok), tok))

        def plane_before(t, _):
            for m in range(group):
                at = pl.ds(pl.multiple_of(t * tok, tok), tok)
                expand(before[m:], at, pl.ds(pl.multiple_of(t * plane + m * tok, tok), tok))
            return 0

        lax.fori_loop(planes - 1 - grp, planes - 1, plane_before, 0)

    m_sc[...] = jnp.full_like(m_sc, NEG_FILL)
    acc_sc[...] = jnp.zeros_like(acc_sc)
    base = pl.multiple_of(block * size, size)

    def step(first, width, query_at=None):
        keys = kv_sc[pl.ds(first, width), :HEAD]
        values = kv_sc[pl.ds(first, width), HEAD:]
        values = jnp.concatenate([values, jnp.ones_like(values)], axis=1)
        scores = []
        for u in range(parts):
            s = lax.dot_general(
                q_sc[pl.ds(base + u * rows, rows), :],
                keys,
                (((1,), (1,)), ((), ())),
                preferred_element_type=jnp.float32,
            )
            if query_at is not None:
                row = lax.broadcasted_iota(jnp.int32, s.shape, 0) + (query_at + u * rows)
                column = lax.broadcasted_iota(jnp.int32, s.shape, 1)
                s = jnp.where(column <= row, s, NEG_FILL)
            scores.append(s)
        for u in range(parts):
            at = slice(u * rows, (u + 1) * rows)
            old = m_sc[at]
            new = jnp.maximum(old, jnp.max(scores[u], axis=1, keepdims=True))
            m_sc[at] = new
            shifted = scores[u] - jnp.tile(new, (1, width // HEAD))
            weights = jnp.exp2(shifted * rate).astype(jnp.bfloat16)
            again = jnp.exp2((old - new) * rate)
            acc_sc[at] = acc_sc[at] * jnp.concatenate([again, again], axis=1) + jnp.dot(
                weights, values, preferred_element_type=jnp.float32
            )

    def plane_step(t, _):
        step(pl.multiple_of(t * plane, plane), plane)
        return 0

    for b in range(plane // size):

        @pl.when(block == b)
        def _():
            step(earlier, (b + 1) * size, b * size)

    lax.fori_loop(planes - 1 - grp, planes - 1, plane_step, 0)
    o_ref[...] = (acc_sc[:, :HEAD] / acc_sc[:, HEAD:]).astype(o_ref.dtype)


def attention(place, queries, own, before, w, first_head, heads):
    planes, group, cols = len(w), len(queries), len(own)
    tok, features = own[0][0].shape
    plane = tok * group
    total = planes * plane
    size = plane // 2
    fixed = lambda h, j, s: (0, 0)
    whole = [pl.BlockSpec(x.shape, fixed, pipeline_mode=pl.Buffered(1)) for x in own[0] * cols]
    whole += [pl.BlockSpec(x.shape, fixed, pipeline_mode=pl.Buffered(1)) for x in before[0] * cols]
    return pl.pallas_call(
        functools.partial(
            attention_kernel,
            planes=planes,
            group=group,
            cols=cols,
            rate=HEAD**-0.5 * math.log2(math.e),
            parts=2,
        ),
        out_shape=jax.ShapeDtypeStruct((plane, heads * HEAD), jnp.bfloat16),
        grid_spec=pltpu.PrefetchScalarGridSpec(
            num_scalar_prefetch=1,
            grid=(heads, plane // size),
            in_specs=[pl.BlockSpec((tok, HEAD), lambda h, j, s: (0, h + first_head)) for _ in queries]
            + whole
            + [
                pl.BlockSpec((*x.shape[:2], 2 * HEAD), lambda h, j, s: (0, 0, h + first_head)) for x in w
            ],
            out_specs=pl.BlockSpec((size, HEAD), lambda h, j, s: (j, h)),
            scratch_shapes=[
                pltpu.VMEM((plane, HEAD), jnp.bfloat16),
                pltpu.VMEM((features * cols, 2 * HEAD), jnp.bfloat16),
                pltpu.VMEM((total, 2 * HEAD), jnp.bfloat16),
                pltpu.VMEM((size, HEAD), jnp.float32),
                pltpu.VMEM((size, 2 * HEAD), jnp.float32),
            ],
        ),
        compiler_params=pltpu.CompilerParams(
            dimension_semantics=("arbitrary", "arbitrary"), vmem_limit_bytes=VMEM_LIMIT
        ),
        cost_estimate=pl.CostEstimate(
            flops=heads * plane * total * HEAD * 6,
            transcendentals=heads * plane * total,
            bytes_accessed=total * features * cols * 2,
        ),
        name="attention",
    )(place, *queries, *(x for some in own for x in some), *(x for some in before for x in some), *w)


def project_kernel(scalars, *refs, counts, group, planes):
    a_refs, refs = refs[: sum(counts)], refs[sum(counts) :]
    b_refs, refs = refs[: planes + 1], refs[planes + 1 :]
    outs, (b_sc, sems) = refs[:group], refs[group:]
    step = pl.program_id(0)
    near = scalars[len(counts) + 1] == 1

    @pl.when(step == 0)
    def _():
        copies = [pltpu.make_async_copy(b_refs[k], b_sc.at[k], sems.at[k]) for k in range(planes - 1)]
        for copy in copies:
            copy.start()
        for which, source in ((near, b_refs[planes - 1]), (jnp.logical_not(near), b_refs[planes])):

            @pl.when(which)
            def _():
                copy = pltpu.make_async_copy(source, b_sc.at[planes - 1], sems.at[planes - 1])
                copy.start()
                copy.wait()

        for copy in copies:
            copy.wait()

    out, at = None, 0
    for x, count in enumerate(counts):
        heads = [a_refs[at + i][...] for i in range(count)]
        a = heads[0] if count == 1 else jnp.concatenate(heads, axis=1)
        term = jnp.dot(a, b_sc[scalars[x]], preferred_element_type=jnp.float32)
        out = term if out is None else out + term
        at += count
    for m in range(group):

        @pl.when(step == m)
        def _():
            outs[m][...] = out.astype(outs[m].dtype)


def project(scalars, sets, blocks, group):
    pieces = [x for some in sets for x in some]
    planes = len(blocks) - 1
    tok = pieces[0].shape[0] // group
    depth, width = blocks[0].shape
    count = len(sets)
    return pl.pallas_call(
        functools.partial(
            project_kernel, counts=[len(some) for some in sets], group=group, planes=planes
        ),
        out_shape=[jax.ShapeDtypeStruct((tok, width), jnp.bfloat16)] * group,
        grid_spec=pltpu.PrefetchScalarGridSpec(
            num_scalar_prefetch=1,
            grid=(group,),
            in_specs=[
                pl.BlockSpec((tok, x.shape[1]), lambda j, s: (s[count] ^ j, 0)) for x in pieces
            ]
            + [pl.BlockSpec(memory_space=pl.ANY) for _ in blocks],
            out_specs=[pl.BlockSpec((tok, width), lambda j, s: (0, 0))] * group,
            scratch_shapes=[
                pltpu.VMEM((planes, depth, width), jnp.bfloat16),
                pltpu.SemaphoreType.DMA((planes,)),
            ],
        ),
        compiler_params=pltpu.CompilerParams(
            dimension_semantics=("arbitrary",), vmem_limit_bytes=VMEM_LIMIT
        ),
        cost_estimate=pl.CostEstimate(
            flops=2 * tok * group * planes * depth * width,
            transcendentals=0,
            bytes_accessed=planes * depth * width * 2 + tok * group * planes * depth * 2,
        ),
        name="project",
    )(scalars, *pieces, *blocks)


def per_device(latent, w_kv, queries, w_out):
    planes, group, cols = lax.axis_size("grp"), lax.axis_size("mem"), lax.axis_size("col")
    grp, mem, col = lax.axis_index("grp"), lax.axis_index("mem"), lax.axis_index("col")
    per_col = queries.shape[1] // HEAD
    run = w_out.shape[0] // HEAD
    turns = per_col // (group * run)
    place = jnp.stack([grp, mem, col]).astype(jnp.int32)
    shifts = range(group)

    def swap(x, m):
        return lax.ppermute(x, "mem", [(p, p ^ m) for p in range(group)])

    def gather(x):
        return [x] + [swap(x, m) for m in range(1, group)]

    def exchange(xs):
        return [xs[0]] + [swap(xs[m], m) for m in range(1, group)]

    def up(x, k):
        return lax.ppermute(x, "grp", [(z, z + k) for z in range(planes - k)])

    def across(x, s):
        return lax.ppermute(x, "col", [((c + s) % cols, c) for c in range(cols)])

    def plane_swap(x, k, senders=None):
        senders = range(planes) if senders is None else senders
        return lax.ppermute(x, "grp", [(z, z ^ k) for z in senders])

    far_shift, half = planes - 1, planes // 2
    near = [z for z in range(planes) if abs(z - (z ^ far_shift)) == 1]
    far = [z for z in range(planes) if z not in near]
    is_near = functools.reduce(jnp.logical_or, [grp == z for z in near]).astype(jnp.int32)

    def relay(x):
        last = far_shift ^ half
        return plane_swap(x, last, [z ^ last for z in far])

    width = w_out.shape[1] // group
    first_width = -(-width // (2 * HEAD)) * HEAD
    spans = [(0, first_width), (first_width, width - first_width)]

    def by_turn(n):
        return [(m, n, [(t * group * n, n) for t in range(turns)]) for m in shifts]

    takes = [
        by_turn(run * 2 * HEAD),
        [(m, width, [span]) for span in spans for m in shifts],
        by_turn(run * HEAD),
    ]
    blocks = cut(place, [w_kv, w_out, queries], takes)
    w_mine = exchange(blocks[:group])
    lower = [up(latent, k) for k in range(planes - 1, 0, -1)]
    own = gather(latent)
    w_first = exchange(blocks[group : 2 * group])

    w_mine = jnp.stack(w_mine)
    w_all = [w_mine] + [plane_swap(w_mine, k) for k in range(1, planes)]

    middle_shifts = [half, *(k for k in range(1, far_shift) if k != half)]

    def spread(x):
        x = jnp.concatenate(x)
        return [x] + [plane_swap(x, k) for k in middle_shifts] + [plane_swap(x, far_shift, near)]

    out_first = spread(w_first)
    q_send, lower, _ = lax.optimization_barrier((blocks[3 * group :], lower, w_first[1:]))
    below = gather(jnp.concatenate(lower))
    my_queries = exchange(q_send)
    w_send, _ = lax.optimization_barrier((blocks[2 * group : 3 * group], my_queries))
    w_second = exchange(w_send)

    owns = [own] + [[across(x, s) for x in own] for s in range(1, cols)]
    belows = [below] + [[across(x, s) for x in below] for s in range(1, cols)]

    calls = [(t, t * run, run) for t in range(turns - 1)]
    calls += [((turns - 1), (turns - 1) * run + i, 1) for i in range(run)]
    results = [[] for _ in range(turns)]
    done = []
    for turn, first_head, heads in calls:
        i = len(done)
        done.append(attention(place, my_queries, owns, belows, w_all, first_head, heads))
        results[turn].append(gather(done[-1]))
        if i == 0:
            w_second, _ = lax.optimization_barrier((w_second, done[0]))
            out_second = spread(w_second)
    middle, _ = lax.optimization_barrier((out_first[1], done[max(len(done) - 2, 0)]))
    first_far = relay(middle)
    middle, _ = lax.optimization_barrier((out_second[1], done[-1]))
    second_far = relay(middle)

    sets, meets = [], []
    for turn in range(turns):
        for s in range(cols):
            some = [[x if s == 0 else across(x, s) for x in part] for part in results[turn]]
            sets.append([part[m] for m in shifts for part in some])
            meets.append((((col + s) % cols) * turns + turn) ^ grp)
    scalars = jnp.stack([*meets, mem, is_near]).astype(jnp.int32)

    def in_order(out, last):
        by_shift = {0: out[0], half: out[1], far_shift: out[-1]}
        by_shift.update(zip(middle_shifts[1:], out[2:-1]))
        return [by_shift[k] for k in range(planes)] + [last]

    mixed = []
    for out, last in ((out_first, first_far), (out_second, second_far)):
        columns = project(scalars, sets, in_order(out, last), group)
        got = exchange(columns)
        stack = jnp.stack(got)
        mixed.append([lax.dynamic_index_in_dim(stack, mem ^ p, 0, False) for p in shifts])
    return jnp.concatenate([part[p] for p in shifts for part in mixed], axis=1)


def solution(mesh):
    rows, cols = mesh.devices.shape
    group = 4
    fine = Mesh(mesh.devices.reshape(rows // group, group, cols), ("grp", "mem", "col"))
    spec = P(("grp", "mem"), "col")

    return jax.shard_map(per_device, mesh=fine, in_specs=(spec,) * 4, out_specs=spec, check_vma=False)
```

profile of v0, /device:TPU:0, one launch (start us, length us, event | category | flops | bytes accessed | tf_op | source)
XLA Modules:
  0.0 366.8 jit_solution(12269738809312811466)
XLA Ops:
  0.0 7.0 %collective-permute-start = (bf16[384,256]{1,0:T(8,128)(2,1)}, bf16[384,256]{1,0:T(8,128)(2,1)S(1)}, u32[]{:S(2)}, u32[]{:S(2)}) collective-permute-start(bf16[384,256]{1,0:T(8,128)(2,1)} %refs_4_.5), channel_id=1, source_target_pairs={{0,24},{1,25},{2,26},{3,27},{4,28},{5,29},{6,30},{7,31}} | collective-permute-start | bytes 589832 | tf_op jit(solution)/shard_map/ppermute | solution.py:294
  7.7 5.1 %cut.1 = (bf16[32,1024]{1,0:T(8,128)(2,1)}, bf16[32,1024]{1,0:T(8,128)(2,1)}, bf16[32,1024]{1,0:T(8,128)(2,1)}, bf16[32,1024]{1,0:T(8,128)(2,1)}, bf16[256,512]{...) custom-call(s32[3]{0:T(128)} %pad_add_fusion.place, ...), custom_call_target="tpu_custom_call" | custom-call | bytes 7340032 | tf_op jit(solution)/shard_map/cut/pallas_call | solution.py:42
  34.3 5.3 %collective-permute-done.4 = bf16[256,512]{1,0:T(8,128)(2,1)S(1)} collective-permute-done((bf16[256,512]{1,0:T(8,128)(2,1)}, bf16[256,512]{1,0:T(8,128)(2,1)S(1)}, u32[]{:S(2)}, u32[]{:S(2)}) %collective-permute-start.4) | collective-permute-done | bytes 262176 | tf_op jit(solution)/shard_map/ppermute | solution.py:285
  45.7 4.5 %collective-permute-done.26.refs_21_ = bf16[4,32,1024]{2,1,0:T(8,128)(2,1)} collective-permute-done((bf16[4,32,1024]{2,1,0:T(8,128)(2,1)S(1)}, bf16[4,32,1024]{2,1,0:T(8,128)(2,1)}, u32[]{:S(2)}, u32[]{:S(2)}) %collective-permute-start.26) | collective-permute-done | bytes 262176 | tf_op jit(solution)/shard_map/ppermute | solution.py:301
  51.1 11.4 %collective-permute-done.27.refs_22_ = bf16[4,32,1024]{2,1,0:T(8,128)(2,1)} collective-permute-done((bf16[4,32,1024]{2,1,0:T(8,128)(2,1)S(1)}, bf16[4,32,1024]{2,1,0:T(8,128)(2,1)}, u32[]{:S(2)}, u32[]{:S(2)}) %collective-permute-start.27) | collective-permute-done | bytes 262176 | tf_op jit(solution)/shard_map/ppermute | solution.py:301
  67.5 18.7 %collective-permute-done.6.refs_1_ = bf16[384,512]{1,0:T(8,128)(2,1)S(1)} collective-permute-done((bf16[384,512]{1,0:T(8,128)(2,1)}, bf16[384,512]{1,0:T(8,128)(2,1)S(1)}, u32[]{:S(2)}, u32[]{:S(2)}) %collective-permute-start.6) | collective-permute-done | bytes 393248 | tf_op jit(solution)/shard_map/ppermute | solution.py:285
  87.1 17.2 %collective-permute-done.7.refs_2_ = bf16[384,512]{1,0:T(8,128)(2,1)S(1)} collective-permute-done((bf16[384,512]{1,0:T(8,128)(2,1)}, bf16[384,512]{1,0:T(8,128)(2,1)S(1)}, u32[]{:S(2)}, u32[]{:S(2)}) %collective-permute-start.7) | collective-permute-done | bytes 393248 | tf_op jit(solution)/shard_map/ppermute | solution.py:285
  105.6 3.4 collective-permute-done.15.refs_11_
  113.6 8.2 %attention.5.refs_9_ = bf16[1536,128]{1,0:T(8,128)(2,1)} custom-call(s32[3]{0:T(128)} %pad_add_fusion.place, bf16[384,512]{1,0:T(8,128)(2,1)} %get-tuple-element.53.refs_0_, bf16[384,512]{1,0:T(8,128)(2,1)} %copy-done.40, bf16[384,512]{1,0:T(8,128)(2,1)} %copy-done.41, bf16[384,512]{1,0:T(8,128)(2,1)} %copy-done.42, bf16[384,256]{1,0:T(8,128)(2,1)} %refs_4_.5, ...), custom_call_target="tpu_custom_call" | custom-call | flops 7247757312 | bytes 6291456 | tf_op jit(solution)/shard_map/attention/pallas_call | solution.py:163
  122.8 11.7 %attention.3.refs_0_ = bf16[1536,256]{1,0:T(8,128)(2,1)} custom-call(s32[3]{0:T(128)} %pad_add_fusion.place, bf16[384,512]{1,0:T(8,128)(2,1)} %get-tuple-element.53.refs_0_, bf16[384,512]{1,0:T(8,128)(2,1)} %copy-done.40, bf16[384,512]{1,0:T(8,128)(2,1)} %copy-done.41, bf16[384,512]{1,0:T(8,128)(2,1)} %copy-done.42, bf16[384,256]{1,0:T(8,128)(2,1)} %refs_4_.5, ...), custom_call_target="tpu_custom_call" | custom-call | flops 14495514624 | bytes 6291456 | tf_op jit(solution)/shard_map/attention/pallas_call | solution.py:163
  134.6 8.4 %attention.4.refs_8_ = bf16[1536,128]{1,0:T(8,128)(2,1)} custom-call(s32[3]{0:T(128)} %pad_add_fusion.place, bf16[384,512]{1,0:T(8,128)(2,1)} %get-tuple-element.53.refs_0_, bf16[384,512]{1,0:T(8,128)(2,1)} %copy-done.40, bf16[384,512]{1,0:T(8,128)(2,1)} %copy-done.41, bf16[384,512]{1,0:T(8,128)(2,1)} %copy-done.42, bf16[384,256]{1,0:T(8,128)(2,1)} %refs_4_.5, ...), custom_call_target="tpu_custom_call" | custom-call | flops 7247757312 | bytes 6291456 | tf_op jit(solution)/shard_map/attention/pallas_call | solution.py:163
  146.7 6.5 %collective-permute-done.51.refs_26_ = bf16[1024,512]{1,0:T(8,128)(2,1)} collective-permute-done((bf16[1024,512]{1,0:T(8,128)(2,1)S(1)}, bf16[1024,512]{1,0:T(8,128)(2,1)}, u32[]{:S(2)}, u32[]{:S(2)}) %collective-permute-start.51) | collective-permute-done | bytes 1048608 | tf_op jit(solution)/shard_map/ppermute | solution.py:301
  155.7 9.6 %collective-permute-done.39.refs_13_ = bf16[1536,128]{1,0:T(8,128)(2,1)S(1)} collective-permute-done((bf16[1536,128]{1,0:T(8,128)(2,1)S(1)}, bf16[1536,128]{1,0:T(8,128)(2,1)S(1)}, u32[]{:S(2)}, u32[]{:S(2)}) %collective-permute-start.39) | collective-permute-done | bytes 393248 | tf_op jit(solution)/shard_map/ppermute | solution.py:285
  165.3 32.4 %collective-permute-start.61 = (bf16[1024,384]{1,0:T(8,128)(2,1)S(1)}, bf16[1024,384]{1,0:T(8,128)(2,1)S(1)}, u32[]{:S(2)}, u32[]{:S(2)}) collective-permute-start(bf16[1024,384]{1,0:T(8,128)(2,1)S(1)} %constant_dynamic-update-slice_fusion.7.refs_24_), channel_id=1, source_target_pairs={{0,16},{8,24},{16,0},{24,8},{1,17},{9,25},{17,1},{25,9},{2,18},{10... | collective-permute-start | bytes 2359304 | tf_op jit(solution)/shard_map/ppermute | solution.py:301
  197.7 10.2 %collective-permute-start.60 = (bf16[1024,384]{1,0:T(8,128)(2,1)S(1)}, bf16[1024,384]{1,0:T(8,128)(2,1)S(1)}, u32[]{:S(2)}, u32[]{:S(2)}) collective-permute-start(bf16[1024,384]{1,0:T(8,128)(2,1)S(1)} %constant_dynamic-update-slice_fusion.7.refs_24_), channel_id=1, source_target_pairs={{0,8},{8,0},{16,24},{24,16},{1,9},{9,1},{17,25},{25,17},{2,10},{10... | collective-permute-start | bytes 2359304 | tf_op jit(solution)/shard_map/ppermute | solution.py:301
  211.7 21.2 %collective-permute-done.61.refs_26_ = bf16[1024,384]{1,0:T(8,128)(2,1)S(1)} collective-permute-done((bf16[1024,384]{1,0:T(8,128)(2,1)S(1)}, bf16[1024,384]{1,0:T(8,128)(2,1)S(1)}, u32[]{:S(2)}, u32[]{:S(2)}) %collective-permute-start.61) | collective-permute-done | bytes 786464 | tf_op jit(solution)/shard_map/ppermute | solution.py:301
  239.6 10.6 %collective-permute-done.29.refs_1_ = bf16[1536,256]{1,0:T(8,128)(2,1)S(1)} collective-permute-done((bf16[1536,256]{1,0:T(8,128)(2,1)S(1)}, bf16[1536,256]{1,0:T(8,128)(2,1)S(1)}, u32[]{:S(2)}, u32[]{:S(2)}) %collective-permute-start.29) | collective-permute-done | bytes 786464 | tf_op jit(solution)/shard_map/ppermute | solution.py:285
  250.2 21.7 %collective-permute-done.30.refs_2_ = bf16[1536,256]{1,0:T(8,128)(2,1)} collective-permute-done((bf16[1536,256]{1,0:T(8,128)(2,1)S(1)}, bf16[1536,256]{1,0:T(8,128)(2,1)}, u32[]{:S(2)}, u32[]{:S(2)}) %collective-permute-start.30) | collective-permute-done | bytes 786464 | tf_op jit(solution)/shard_map/ppermute | solution.py:285
  272.4 10.3 %collective-permute-start.50 = (bf16[1024,512]{1,0:T(8,128)(2,1)S(1)}, bf16[1024,512]{1,0:T(8,128)(2,1)S(1)}, u32[]{:S(2)}, u32[]{:S(2)}) collective-permute-start(bf16[1024,512]{1,0:T(8,128)(2,1)S(1)} %constant_dynamic-update-slice_fusion.3.refs_24_), channel_id=1, source_target_pairs={{0,8},{8,0},{16,24},{24,16},{1,9},{9,1},{17,25},{25,17},{2,10},{10... | collective-permute-start | bytes 3145736 | tf_op jit(solution)/shard_map/ppermute | solution.py:301
  287.3 14.8 %project.3 = (bf16[384,384]{1,0:T(8,128)(2,1)}, bf16[384,384]{1,0:T(8,128)(2,1)}, bf16[384,384]{1,0:T(8,128)(2,1)}, bf16[384,384]{1,0:T(8,128)(2,1)}) custom-call(s32[6]{0:T(128)} %stack.86.scalars, bf16[1536,256]{1,0:T(8,128)(2,1)} %attention.3.refs_0_, bf16[1536,256]{1,0:T(8,128)(2,1)} %copy-done.12, bf16[1536,256]{1,0:T(8,128)(2,1)} %collective-permute-done.30.refs_2_, ...), custom_call_target="tpu_custom_call" | custom-call | flops 4831838208 | bytes 15728640 | tf_op jit(solution)/shard_map/project/pallas_call | solution.py:245
  310.3 18.2 %collective-permute-done.53.refs_28_ = bf16[1024,512]{1,0:T(8,128)(2,1)} collective-permute-done((bf16[1024,512]{1,0:T(8,128)(2,1)}, bf16[1024,512]{1,0:T(8,128)(2,1)}, u32[]{:S(2)}, u32[]{:S(2)}) %collective-permute-start.53) | collective-permute-done | bytes 1048608 | tf_op jit(solution)/shard_map/ppermute | solution.py:301
  328.6 14.9 %project.2 = (bf16[384,512]{1,0:T(8,128)(2,1)}, bf16[384,512]{1,0:T(8,128)(2,1)}, bf16[384,512]{1,0:T(8,128)(2,1)}, bf16[384,512]{1,0:T(8,128)(2,1)}) custom-call(s32[6]{0:T(128)} %stack.86.scalars, bf16[1536,256]{1,0:T(8,128)(2,1)} %attention.3.refs_0_, bf16[1536,256]{1,0:T(8,128)(2,1)} %copy-done.12, bf16[1536,256]{1,0:T(8,128)(2,1)} %collective-permute-done.30.refs_2_, ...), custom_call_target="tpu_custom_call" | custom-call | flops 6442450944 | bytes 16777216 | tf_op jit(solution)/shard_map/project/pallas_call | solution.py:245
  347.3 8.5 %collective-permute-done.54 = bf16[384,512]{1,0:T(8,128)(2,1)S(1)} collective-permute-done((bf16[384,512]{1,0:T(8,128)(2,1)}, bf16[384,512]{1,0:T(8,128)(2,1)S(1)}, u32[]{:S(2)}, u32[]{:S(2)}) %collective-permute-start.54) | collective-permute-done | bytes 393248 | tf_op jit(solution)/shard_map/ppermute | solution.py:285
  355.8 8.1 %collective-permute-done.55 = bf16[384,512]{1,0:T(8,128)(2,1)S(1)} collective-permute-done((bf16[384,512]{1,0:T(8,128)(2,1)}, bf16[384,512]{1,0:T(8,128)(2,1)S(1)}, u32[]{:S(2)}, u32[]{:S(2)}) %collective-permute-start.55) | collective-permute-done | bytes 393248 | tf_op jit(solution)/shard_map/ppermute | solution.py:285
  (242 shorter events, 78.2 us)
Async XLA Ops:
  50.2 54.0 %collective-permute-start.16 = (bf16[1152,256]{1,0:T(8,128)(2,1)S(1)}, bf16[1152,256]{1,0:T(8,128)(2,1)S(1)}, u32[]{:S(2)}, u32[]{:S(2)}) collective-permute-start(bf16[1152,256]{1,0:T(8,128)(2,1)S(1)} %constant_dynamic-update-slice_fusion.refs_12_), channel_id=1, source_target_pairs={{0,2},{2,0},{4,6},{6,4},{1,3},{3,1},{5,7},{7,5},{8,10},{10,8},{12,... | collective-permute-start | bytes 1769480 | tf_op jit(solution)/shard_map/ppermute | solution.py:285
  62.5 42.3 %collective-permute-start.17 = (bf16[1152,256]{1,0:T(8,128)(2,1)S(1)}, bf16[1152,256]{1,0:T(8,128)(2,1)S(1)}, u32[]{:S(2)}, u32[]{:S(2)}) collective-permute-start(bf16[1152,256]{1,0:T(8,128)(2,1)S(1)} %constant_dynamic-update-slice_fusion.refs_12_), channel_id=1, source_target_pairs={{0,4},{2,6},{4,0},{6,2},{1,5},{3,7},{5,1},{7,3},{8,12},{10,14},{12... | collective-permute-start | bytes 1769480 | tf_op jit(solution)/shard_map/ppermute | solution.py:285
  64.0 40.9 %collective-permute-start.18 = (bf16[1152,256]{1,0:T(8,128)(2,1)S(1)}, bf16[1152,256]{1,0:T(8,128)(2,1)S(1)}, u32[]{:S(2)}, u32[]{:S(2)}) collective-permute-start(bf16[1152,256]{1,0:T(8,128)(2,1)S(1)} %constant_dynamic-update-slice_fusion.refs_12_), channel_id=1, source_target_pairs={{0,6},{2,4},{4,2},{6,0},{1,7},{3,5},{5,3},{7,1},{8,14},{10,12},{12... | collective-permute-start | bytes 1769480 | tf_op jit(solution)/shard_map/ppermute | solution.py:285
  66.0 38.2 %collective-permute-start.7 = (bf16[384,512]{1,0:T(8,128)(2,1)}, bf16[384,512]{1,0:T(8,128)(2,1)S(1)}, u32[]{:S(2)}, u32[]{:S(2)}) collective-permute-start(bf16[384,512]{1,0:T(8,128)(2,1)} %get-tuple-element.55), channel_id=1, source_target_pairs={{0,4},{2,6},{4,0},{6,2},{1,5},{3,7},{5,1},{7,3},{8,12},{10,14},{12... | collective-permute-start | bytes 1179656 | tf_op jit(solution)/shard_map/ppermute | solution.py:285
  109.0 44.1 %collective-permute-start.51 = (bf16[1024,512]{1,0:T(8,128)(2,1)S(1)}, bf16[1024,512]{1,0:T(8,128)(2,1)}, u32[]{:S(2)}, u32[]{:S(2)}) collective-permute-start(bf16[1024,512]{1,0:T(8,128)(2,1)S(1)} %constant_dynamic-update-slice_fusion.3.refs_24_), channel_id=1, source_target_pairs={{0,16},{8,24},{16,0},{24,8},{1,17},{9,25},{17,1},{25,9},{2,18},{10... | collective-permute-start | bytes 3145736 | tf_op jit(solution)/shard_map/ppermute | solution.py:301
  109.1 33.9 %collective-permute-start.57 = (bf16[256,384]{1,0:T(8,128)(2,1)}, bf16[256,384]{1,0:T(8,128)(2,1)S(1)}, u32[]{:S(2)}, u32[]{:S(2)}) collective-permute-start(bf16[256,384]{1,0:T(8,128)(2,1)} %get-tuple-element.75), channel_id=1, source_target_pairs={{0,2},{2,0},{4,6},{6,4},{1,3},{3,1},{5,7},{7,5},{8,10},{10,8},{12,... | collective-permute-start | bytes 589832 | tf_op jit(solution)/shard_map/ppermute | solution.py:285
  110.1 33.8 %collective-permute-start.58 = (bf16[256,384]{1,0:T(8,128)(2,1)}, bf16[256,384]{1,0:T(8,128)(2,1)S(1)}, u32[]{:S(2)}, u32[]{:S(2)}) collective-permute-start(bf16[256,384]{1,0:T(8,128)(2,1)} %get-tuple-element.76), channel_id=1, source_target_pairs={{0,4},{2,6},{4,0},{6,2},{1,5},{3,7},{5,1},{7,3},{8,12},{10,14},{12... | collective-permute-start | bytes 589832 | tf_op jit(solution)/shard_map/ppermute | solution.py:285
  111.0 34.6 %collective-permute-start.59 = (bf16[256,384]{1,0:T(8,128)(2,1)}, bf16[256,384]{1,0:T(8,128)(2,1)S(1)}, u32[]{:S(2)}, u32[]{:S(2)}) collective-permute-start(bf16[256,384]{1,0:T(8,128)(2,1)} %get-tuple-element.77), channel_id=1, source_target_pairs={{0,6},{2,4},{4,2},{6,0},{1,7},{3,5},{5,3},{7,1},{8,14},{10,12},{12... | collective-permute-start | bytes 589832 | tf_op jit(solution)/shard_map/ppermute | solution.py:285
  143.9 53.7 %collective-permute-start.41 = (bf16[1536,128]{1,0:T(8,128)(2,1)S(1)}, bf16[1536,128]{1,0:T(8,128)(2,1)S(1)}, u32[]{:S(2)}, u32[]{:S(2)}) collective-permute-start(bf16[1536,128]{1,0:T(8,128)(2,1)S(1)} %copy-done.25), channel_id=1, source_target_pairs={{0,6},{2,4},{4,2},{6,0},{1,7},{3,5},{5,3},{7,1},{8,14},{10,12},{12... | collective-permute-start | bytes 1179656 | tf_op jit(solution)/shard_map/ppermute | solution.py:285
  145.6 62.2 %collective-permute-start.36 = (bf16[1536,128]{1,0:T(8,128)(2,1)}, bf16[1536,128]{1,0:T(8,128)(2,1)S(1)}, u32[]{:S(2)}, u32[]{:S(2)}) collective-permute-start(bf16[1536,128]{1,0:T(8,128)(2,1)} %attention.4.refs_8_), channel_id=1, source_target_pairs={{0,2},{2,0},{4,6},{6,4},{1,3},{3,1},{5,7},{7,5},{8,10},{10,8},{12,... | collective-permute-start | bytes 1179656 | tf_op jit(solution)/shard_map/ppermute | solution.py:285
  153.2 55.3 %collective-permute-start.38 = (bf16[1536,128]{1,0:T(8,128)(2,1)}, bf16[1536,128]{1,0:T(8,128)(2,1)S(1)}, u32[]{:S(2)}, u32[]{:S(2)}) collective-permute-start(bf16[1536,128]{1,0:T(8,128)(2,1)} %attention.4.refs_8_), channel_id=1, source_target_pairs={{0,4},{2,6},{4,0},{6,2},{1,5},{3,7},{5,1},{7,3},{8,12},{10,14},{12... | collective-permute-start | bytes 1179656 | tf_op jit(solution)/shard_map/ppermute | solution.py:285
  154.0 54.7 %collective-permute-start.40 = (bf16[1536,128]{1,0:T(8,128)(2,1)}, bf16[1536,128]{1,0:T(8,128)(2,1)S(1)}, u32[]{:S(2)}, u32[]{:S(2)}) collective-permute-start(bf16[1536,128]{1,0:T(8,128)(2,1)} %attention.4.refs_8_), channel_id=1, source_target_pairs={{0,6},{2,4},{4,2},{6,0},{1,7},{3,5},{5,3},{7,1},{8,14},{10,12},{12... | collective-permute-start | bytes 1179656 | tf_op jit(solution)/shard_map/ppermute | solution.py:285
  165.3 67.6 %collective-permute-start.61 = (bf16[1024,384]{1,0:T(8,128)(2,1)S(1)}, bf16[1024,384]{1,0:T(8,128)(2,1)S(1)}, u32[]{:S(2)}, u32[]{:S(2)}) collective-permute-start(bf16[1024,384]{1,0:T(8,128)(2,1)S(1)} %constant_dynamic-update-slice_fusion.7.refs_24_), channel_id=1, source_target_pairs={{0,16},{8,24},{16,0},{24,8},{1,17},{9,25},{17,1},{25,9},{2,18},{10... | collective-permute-start | bytes 2359304 | tf_op jit(solution)/shard_map/ppermute | solution.py:301
  197.7 35.9 %collective-permute-start.60 = (bf16[1024,384]{1,0:T(8,128)(2,1)S(1)}, bf16[1024,384]{1,0:T(8,128)(2,1)S(1)}, u32[]{:S(2)}, u32[]{:S(2)}) collective-permute-start(bf16[1024,384]{1,0:T(8,128)(2,1)S(1)} %constant_dynamic-update-slice_fusion.7.refs_24_), channel_id=1, source_target_pairs={{0,8},{8,0},{16,24},{24,16},{1,9},{9,1},{17,25},{25,17},{2,10},{10... | collective-permute-start | bytes 2359304 | tf_op jit(solution)/shard_map/ppermute | solution.py:301
  235.3 36.5 %collective-permute-start.30 = (bf16[1536,256]{1,0:T(8,128)(2,1)S(1)}, bf16[1536,256]{1,0:T(8,128)(2,1)}, u32[]{:S(2)}, u32[]{:S(2)}) collective-permute-start(bf16[1536,256]{1,0:T(8,128)(2,1)S(1)} %copy-done.10), channel_id=1, source_target_pairs={{0,4},{2,6},{4,0},{6,2},{1,5},{3,7},{5,1},{7,3},{8,12},{10,14},{12... | collective-permute-start | bytes 2359304 | tf_op jit(solution)/shard_map/ppermute | solution.py:285
  236.9 35.0 %collective-permute-start.31 = (bf16[1536,256]{1,0:T(8,128)(2,1)S(1)}, bf16[1536,256]{1,0:T(8,128)(2,1)}, u32[]{:S(2)}, u32[]{:S(2)}) collective-permute-start(bf16[1536,256]{1,0:T(8,128)(2,1)S(1)} %copy-done.10), channel_id=1, source_target_pairs={{0,6},{2,4},{4,2},{6,0},{1,7},{3,5},{5,3},{7,1},{8,14},{10,12},{12... | collective-permute-start | bytes 2359304 | tf_op jit(solution)/shard_map/ppermute | solution.py:285
  238.2 34.2 %collective-permute-start.32 = (bf16[1536,256]{1,0:T(8,128)(2,1)S(1)}, bf16[1536,256]{1,0:T(8,128)(2,1)S(1)}, u32[]{:S(2)}, u32[]{:S(2)}) collective-permute-start(bf16[1536,256]{1,0:T(8,128)(2,1)S(1)} %copy-done.10), channel_id=1, source_target_pairs={{1,0},{0,1},{3,2},{2,3},{5,4},{4,5},{7,6},{6,7},{9,8},{8,9},{11,10... | collective-permute-start | bytes 2359304 | tf_op jit(solution)/shard_map/ppermute | solution.py:297
  238.3 44.4 %collective-permute-start.63 = (bf16[1024,384]{1,0:T(8,128)(2,1)S(1)}, bf16[1024,384]{1,0:T(8,128)(2,1)S(1)}, u32[]{:S(2)}, u32[]{:S(2)}) collective-permute-start(bf16[1024,384]{1,0:T(8,128)(2,1)S(1)} %collective-permute-done.61.refs_26_), channel_id=1, source_target_pairs={{8,0},{16,24},{9,1},{17,25},{10,2},{18,26},{11,3},{19,27},{12,4},{... | collective-permute-start | bytes 2359304 | tf_op jit(solution)/shard_map/ppermute | solution.py:301
  250.2 34.1 %collective-permute-start.33 = (bf16[1536,256]{1,0:T(8,128)(2,1)S(1)}, bf16[1536,256]{1,0:T(8,128)(2,1)S(1)}, u32[]{:S(2)}, u32[]{:S(2)}) collective-permute-start(bf16[1536,256]{1,0:T(8,128)(2,1)S(1)} %collective-permute-done.29.refs_1_), channel_id=1, source_target_pairs={{1,0},{0,1},{3,2},{2,3},{5,4},{4,5},{7,6},{6,7},{9,8},{8,9},{11,10... | collective-permute-start | bytes 2359304 | tf_op jit(solution)/shard_map/ppermute | solution.py:297
  272.4 34.3 %collective-permute-start.50 = (bf16[1024,512]{1,0:T(8,128)(2,1)S(1)}, bf16[1024,512]{1,0:T(8,128)(2,1)S(1)}, u32[]{:S(2)}, u32[]{:S(2)}) collective-permute-start(bf16[1024,512]{1,0:T(8,128)(2,1)S(1)} %constant_dynamic-update-slice_fusion.3.refs_24_), channel_id=1, source_target_pairs={{0,8},{8,0},{16,24},{24,16},{1,9},{9,1},{17,25},{25,17},{2,10},{10... | collective-permute-start | bytes 3145736 | tf_op jit(solution)/shard_map/ppermute | solution.py:301
  285.3 43.3 %collective-permute-start.53 = (bf16[1024,512]{1,0:T(8,128)(2,1)}, bf16[1024,512]{1,0:T(8,128)(2,1)}, u32[]{:S(2)}, u32[]{:S(2)}) collective-permute-start(bf16[1024,512]{1,0:T(8,128)(2,1)} %collective-permute-done.51.refs_26_), channel_id=1, source_target_pairs={{8,0},{16,24},{9,1},{17,25},{10,2},{18,26},{11,3},{19,27},{12,4},{... | collective-permute-start | bytes 3145736 | tf_op jit(solution)/shard_map/ppermute | solution.py:301
  302.1 44.8 %collective-permute-start.64 = (bf16[384,384]{1,0:T(8,128)(2,1)}, bf16[384,384]{1,0:T(8,128)(2,1)S(1)}, u32[]{:S(2)}, u32[]{:S(2)}) collective-permute-start(bf16[384,384]{1,0:T(8,128)(2,1)} %get-tuple-element.84), channel_id=1, source_target_pairs={{0,2},{2,0},{4,6},{6,4},{1,3},{3,1},{5,7},{7,5},{8,10},{10,8},{12,... | collective-permute-start | bytes 884744 | tf_op jit(solution)/shard_map/ppermute | solution.py:285
  303.7 43.4 %collective-permute-start.65 = (bf16[384,384]{1,0:T(8,128)(2,1)}, bf16[384,384]{1,0:T(8,128)(2,1)S(1)}, u32[]{:S(2)}, u32[]{:S(2)}) collective-permute-start(bf16[384,384]{1,0:T(8,128)(2,1)} %get-tuple-element.85), channel_id=1, source_target_pairs={{0,4},{2,6},{4,0},{6,2},{1,5},{3,7},{5,1},{7,3},{8,12},{10,14},{12... | collective-permute-start | bytes 884744 | tf_op jit(solution)/shard_map/ppermute | solution.py:285
  307.6 39.5 %collective-permute-start.66 = (bf16[384,384]{1,0:T(8,128)(2,1)}, bf16[384,384]{1,0:T(8,128)(2,1)S(1)}, u32[]{:S(2)}, u32[]{:S(2)}) collective-permute-start(bf16[384,384]{1,0:T(8,128)(2,1)} %get-tuple-element.86), channel_id=1, source_target_pairs={{0,6},{2,4},{4,2},{6,0},{1,7},{3,5},{5,3},{7,1},{8,14},{10,12},{12... | collective-permute-start | bytes 884744 | tf_op jit(solution)/shard_map/ppermute | solution.py:285
  (94 other events, 2439.8 us)
where the time goes:
time: 367 us
  waiting for transfers between devices  179 us (49%)
  starting transfers between devices  115 us (31%)
  Pallas kernels  63.1 us (17%)
  local copies, waits for them, and re-layouts  6.92 us (2%)
    ppermute x33, waiting for transfers between devices, swap(): return lax.ppermute(x, 'mem', [(p, p ^ m) for p in range(group)])  110 us
    ppermute x11, waiting for transfers between devices, plane_swap(): return lax.ppermute(x, 'grp', [(z, z ^ k) for z in senders])  63.1 us
    ppermute x11, starting transfers between devices, plane_swap(): return lax.ppermute(x, 'grp', [(z, z ^ k) for z in senders])  58.1 us
    ppermute x33, starting transfers between devices, swap(): return lax.ppermute(x, 'mem', [(p, p ^ m) for p in range(group)])  41.7 us
    pallas_call x2, Pallas kernels, project(): pl.pallas_call(functools.partial(project_kernel, counts=[len(some) for so...  29.7 us
    pallas_call x3, Pallas kernels, attention(): pl.pallas_call(functools.partial(attention_kernel, planes=planes, group=g...  28.3 us
    ppermute x3, starting transfers between devices, up(): return lax.ppermute(x, 'grp', [(z, z + k) for z in range(planes - k)])  10.7 us
  transfers between devices with their start and end apart: 67, of which 22 were waited for; matrix products, arithmetic and copies ran while one was open for 1% of the time, Pallas kernels for 17%

commit v1 on v0

--- a/solution.py
+++ b/solution.py
@@ -337,11 +337,9 @@
         return [x] + [plane_swap(x, k) for k in middle_shifts] + [plane_swap(x, far_shift, near)]
 
     out_first = spread(w_first)
-    q_send, lower, _ = lax.optimization_barrier((blocks[3 * group :], lower, w_first[1:]))
     below = gather(jnp.concatenate(lower))
-    my_queries = exchange(q_send)
-    w_send, _ = lax.optimization_barrier((blocks[2 * group : 3 * group], my_queries))
-    w_second = exchange(w_send)
+    my_queries = exchange(blocks[3 * group :])
+    w_second = exchange(blocks[2 * group : 3 * group])
 
     owns = [own] + [[across(x, s) for x in own] for s in range(1, cols)]
     belows = [below] + [[across(x, s) for x in below] for s in range(1, cols)]

time: 367 us -> 359 us (0.978)
  waiting for transfers between devices: 179 us -> 155 us
  starting transfers between devices: 115 us -> 130 us
    ppermute x33, waiting for transfers between devices: 110 us -> 93.3 us  [swap(): return lax.ppermute(x, 'mem', [(p, p ^ m) for p in range(group)])]
    ppermute x11, starting transfers between devices: 58.1 us -> 74.5 us  [plane_swap(): return lax.ppermute(x, 'grp', [(z, z ^ k) for z in senders])]
    ppermute x11, waiting for transfers between devices: 63.1 us -> 54.4 us  [plane_swap(): return lax.ppermute(x, 'grp', [(z, z ^ k) for z in senders])]
  transfers between devices with their start and end apart: 67 -> 67, of which waited for: 22 -> 24; matrix products, arithmetic and copies ran while one was open for 1% -> 1% of each run, Pallas kernels for 17% -> 16%
where the time goes in v1:
time: 359 us; the launch traced here: 358 us
  waiting for transfers between devices  155 us (43%)
  starting transfers between devices  130 us (36%)
  Pallas kernels  63.1 us (18%)
  local copies, waits for them, and re-layouts  7.97 us (2%)
    ppermute x33, waiting for transfers between devices, swap(): return lax.ppermute(x, 'mem', [(p, p ^ m) for p in range(group)])  93.3 us
    ppermute x11, starting transfers between devices, plane_swap(): return lax.ppermute(x, 'grp', [(z, z ^ k) for z in senders])  74.5 us
    ppermute x11, waiting for transfers between devices, plane_swap(): return lax.ppermute(x, 'grp', [(z, z ^ k) for z in senders])  54.4 us
    ppermute x33, starting transfers between devices, swap(): return lax.ppermute(x, 'mem', [(p, p ^ m) for p in range(group)])  41.6 us
    pallas_call x2, Pallas kernels, project(): pl.pallas_call(functools.partial(project_kernel, counts=[len(some) for so...  29.7 us
    pallas_call x3, Pallas kernels, attention(): pl.pallas_call(functools.partial(attention_kernel, planes=planes, group=g...  28.3 us
    ppermute x3, starting transfers between devices, up(): return lax.ppermute(x, 'grp', [(z, z + k) for z in range(planes - k)])  9.28 us
  transfers between devices with their start and end apart: 67, of which 24 were waited for; matrix products, arithmetic and copies ran while one was open for 1% of the time, Pallas kernels for 16%

profile of v1, /device:TPU:0, one launch (start us, length us, event | category | flops | bytes accessed | tf_op | source)
XLA Modules:
  0.0 358.2 jit_solution(12052382698766529907)
XLA Ops:
  0.6 5.1 %cut.1 = (bf16[32,1024]{1,0:T(8,128)(2,1)}, bf16[32,1024]{1,0:T(8,128)(2,1)}, bf16[32,1024]{1,0:T(8,128)(2,1)}, bf16[32,1024]{1,0:T(8,128)(2,1)}, bf16[256,512]{...) custom-call(s32[3]{0:T(128)} %pad_add_fusion.place, ...), custom_call_target="tpu_custom_call" | custom-call | bytes 7340032 | tf_op jit(solution)/shard_map/cut/pallas_call | solution.py:42
  5.7 3.1 collective-permute-start.21
  8.7 5.5 %collective-permute-start.10 = (bf16[384,256]{1,0:T(8,128)(2,1)S(1)}, bf16[384,256]{1,0:T(8,128)(2,1)S(1)}, u32[]{:S(2)}, u32[]{:S(2)}) collective-permute-start(bf16[384,256]{1,0:T(8,128)(2,1)S(1)} %copy-done.44), channel_id=1, source_target_pairs={{0,24},{1,25},{2,26},{3,27},{4,28},{5,29},{6,30},{7,31}} | collective-permute-start | bytes 589832 | tf_op jit(solution)/shard_map/ppermute | solution.py:294
  20.1 5.2 %collective-permute-done.22 = bf16[32,1024]{1,0:T(8,128)(2,1)S(1)} collective-permute-done((bf16[32,1024]{1,0:T(8,128)(2,1)}, bf16[32,1024]{1,0:T(8,128)(2,1)S(1)}, u32[]{:S(2)}, u32[]{:S(2)}) %collective-permute-start.22) | collective-permute-done | bytes 65568 | tf_op jit(solution)/shard_map/ppermute | solution.py:285
  52.9 7.8 %collective-permute-done.24.refs_22_ = bf16[4,32,1024]{2,1,0:T(8,128)(2,1)} collective-permute-done((bf16[4,32,1024]{2,1,0:T(8,128)(2,1)S(1)}, bf16[4,32,1024]{2,1,0:T(8,128)(2,1)}, u32[]{:S(2)}, u32[]{:S(2)}) %collective-permute-start.24) | collective-permute-done | bytes 262176 | tf_op jit(solution)/shard_map/ppermute | solution.py:301
  64.2 29.3 %collective-permute-done.1.refs_2_ = bf16[384,512]{1,0:T(8,128)(2,1)S(1)} collective-permute-done((bf16[384,512]{1,0:T(8,128)(2,1)}, bf16[384,512]{1,0:T(8,128)(2,1)S(1)}, u32[]{:S(2)}, u32[]{:S(2)}) %collective-permute-start.1) | collective-permute-done | bytes 393248 | tf_op jit(solution)/shard_map/ppermute | solution.py:285
  107.4 8.2 %attention.5.refs_9_ = bf16[1536,128]{1,0:T(8,128)(2,1)} custom-call(s32[3]{0:T(128)} %pad_add_fusion.place, bf16[384,512]{1,0:T(8,128)(2,1)} %get-tuple-element.35.refs_0_, bf16[384,512]{1,0:T(8,128)(2,1)} %copy-done.40, bf16[384,512]{1,0:T(8,128)(2,1)} %copy-done.41, bf16[384,512]{1,0:T(8,128)(2,1)} %copy-done.42, bf16[384,256]{1,0:T(8,128)(2,1)} %refs_4_.5, ...), custom_call_target="tpu_custom_call" | custom-call | flops 7247757312 | bytes 6291456 | tf_op jit(solution)/shard_map/attention/pallas_call | solution.py:163
  117.5 11.7 %attention.3.refs_0_ = bf16[1536,256]{1,0:T(8,128)(2,1)} custom-call(s32[3]{0:T(128)} %pad_add_fusion.place, bf16[384,512]{1,0:T(8,128)(2,1)} %get-tuple-element.35.refs_0_, bf16[384,512]{1,0:T(8,128)(2,1)} %copy-done.40, bf16[384,512]{1,0:T(8,128)(2,1)} %copy-done.41, bf16[384,512]{1,0:T(8,128)(2,1)} %copy-done.42, bf16[384,256]{1,0:T(8,128)(2,1)} %refs_4_.5, ...), custom_call_target="tpu_custom_call" | custom-call | flops 14495514624 | bytes 6291456 | tf_op jit(solution)/shard_map/attention/pallas_call | solution.py:163
  129.3 8.4 %attention.4.refs_8_ = bf16[1536,128]{1,0:T(8,128)(2,1)} custom-call(s32[3]{0:T(128)} %pad_add_fusion.place, bf16[384,512]{1,0:T(8,128)(2,1)} %get-tuple-element.35.refs_0_, bf16[384,512]{1,0:T(8,128)(2,1)} %copy-done.40, bf16[384,512]{1,0:T(8,128)(2,1)} %copy-done.41, bf16[384,512]{1,0:T(8,128)(2,1)} %copy-done.42, bf16[384,256]{1,0:T(8,128)(2,1)} %refs_4_.5, ...), custom_call_target="tpu_custom_call" | custom-call | flops 7247757312 | bytes 6291456 | tf_op jit(solution)/shard_map/attention/pallas_call | solution.py:163
  141.4 10.7 %collective-permute-done.51.refs_26_ = bf16[1024,512]{1,0:T(8,128)(2,1)} collective-permute-done((bf16[1024,512]{1,0:T(8,128)(2,1)S(1)}, bf16[1024,512]{1,0:T(8,128)(2,1)}, u32[]{:S(2)}, u32[]{:S(2)}) %collective-permute-start.51) | collective-permute-done | bytes 1048608 | tf_op jit(solution)/shard_map/ppermute | solution.py:301
  155.3 3.4 collective-permute-done.36.refs_13_
  158.8 30.3 %collective-permute-start.61 = (bf16[1024,384]{1,0:T(8,128)(2,1)S(1)}, bf16[1024,384]{1,0:T(8,128)(2,1)S(1)}, u32[]{:S(2)}, u32[]{:S(2)}) collective-permute-start(bf16[1024,384]{1,0:T(8,128)(2,1)S(1)} %constant_dynamic-update-slice_fusion.7.refs_24_), channel_id=1, source_target_pairs={{0,16},{8,24},{16,0},{24,8},{1,17},{9,25},{17,1},{25,9},{2,18},{10... | collective-permute-start | bytes 2359304 | tf_op jit(solution)/shard_map/ppermute | solution.py:301
  189.1 16.1 %collective-permute-start.60 = (bf16[1024,384]{1,0:T(8,128)(2,1)S(1)}, bf16[1024,384]{1,0:T(8,128)(2,1)S(1)}, u32[]{:S(2)}, u32[]{:S(2)}) collective-permute-start(bf16[1024,384]{1,0:T(8,128)(2,1)S(1)} %constant_dynamic-update-slice_fusion.7.refs_24_), channel_id=1, source_target_pairs={{0,8},{8,0},{16,24},{24,16},{1,9},{9,1},{17,25},{25,17},{2,10},{10... | collective-permute-start | bytes 2359304 | tf_op jit(solution)/shard_map/ppermute | solution.py:301
  209.0 10.8 %collective-permute-done.61.refs_26_ = bf16[1024,384]{1,0:T(8,128)(2,1)S(1)} collective-permute-done((bf16[1024,384]{1,0:T(8,128)(2,1)S(1)}, bf16[1024,384]{1,0:T(8,128)(2,1)S(1)}, u32[]{:S(2)}, u32[]{:S(2)}) %collective-permute-start.61) | collective-permute-done | bytes 786464 | tf_op jit(solution)/shard_map/ppermute | solution.py:301
  226.5 11.6 %collective-permute-done.26.refs_1_ = bf16[1536,256]{1,0:T(8,128)(2,1)S(1)} collective-permute-done((bf16[1536,256]{1,0:T(8,128)(2,1)S(1)}, bf16[1536,256]{1,0:T(8,128)(2,1)S(1)}, u32[]{:S(2)}, u32[]{:S(2)}) %collective-permute-start.26) | collective-permute-done | bytes 786464 | tf_op jit(solution)/shard_map/ppermute | solution.py:285
  238.1 20.1 %collective-permute-done.27.refs_2_ = bf16[1536,256]{1,0:T(8,128)(2,1)} collective-permute-done((bf16[1536,256]{1,0:T(8,128)(2,1)S(1)}, bf16[1536,256]{1,0:T(8,128)(2,1)}, u32[]{:S(2)}, u32[]{:S(2)}) %collective-permute-start.27) | collective-permute-done | bytes 786464 | tf_op jit(solution)/shard_map/ppermute | solution.py:285
  258.7 16.6 %collective-permute-start.50 = (bf16[1024,512]{1,0:T(8,128)(2,1)S(1)}, bf16[1024,512]{1,0:T(8,128)(2,1)S(1)}, u32[]{:S(2)}, u32[]{:S(2)}) collective-permute-start(bf16[1024,512]{1,0:T(8,128)(2,1)S(1)} %constant_dynamic-update-slice_fusion.3.refs_24_), channel_id=1, source_target_pairs={{0,8},{8,0},{16,24},{24,16},{1,9},{9,1},{17,25},{25,17},{2,10},{10... | collective-permute-start | bytes 3145736 | tf_op jit(solution)/shard_map/ppermute | solution.py:301
  279.9 14.8 %project.3 = (bf16[384,384]{1,0:T(8,128)(2,1)}, bf16[384,384]{1,0:T(8,128)(2,1)}, bf16[384,384]{1,0:T(8,128)(2,1)}, bf16[384,384]{1,0:T(8,128)(2,1)}) custom-call(s32[6]{0:T(128)} %stack.86.scalars, bf16[1536,256]{1,0:T(8,128)(2,1)} %attention.3.refs_0_, bf16[1536,256]{1,0:T(8,128)(2,1)} %copy-done.12, bf16[1536,256]{1,0:T(8,128)(2,1)} %collective-permute-done.27.refs_2_, ...), custom_call_target="tpu_custom_call" | custom-call | flops 4831838208 | bytes 15728640 | tf_op jit(solution)/shard_map/project/pallas_call | solution.py:245
  295.1 4.1 %collective-permute-done.50.refs_25_ = bf16[1024,512]{1,0:T(8,128)(2,1)S(1)} collective-permute-done((bf16[1024,512]{1,0:T(8,128)(2,1)S(1)}, bf16[1024,512]{1,0:T(8,128)(2,1)S(1)}, u32[]{:S(2)}, u32[]{:S(2)}) %collective-permute-start.50) | collective-permute-done | bytes 1048608 | tf_op jit(solution)/shard_map/ppermute | solution.py:301
  300.3 20.9 %collective-permute-done.53.refs_28_ = bf16[1024,512]{1,0:T(8,128)(2,1)} collective-permute-done((bf16[1024,512]{1,0:T(8,128)(2,1)}, bf16[1024,512]{1,0:T(8,128)(2,1)}, u32[]{:S(2)}, u32[]{:S(2)}) %collective-permute-start.53) | collective-permute-done | bytes 1048608 | tf_op jit(solution)/shard_map/ppermute | solution.py:301
  321.2 14.9 %project.2 = (bf16[384,512]{1,0:T(8,128)(2,1)}, bf16[384,512]{1,0:T(8,128)(2,1)}, bf16[384,512]{1,0:T(8,128)(2,1)}, bf16[384,512]{1,0:T(8,128)(2,1)}) custom-call(s32[6]{0:T(128)} %stack.86.scalars, bf16[1536,256]{1,0:T(8,128)(2,1)} %attention.3.refs_0_, bf16[1536,256]{1,0:T(8,128)(2,1)} %copy-done.12, bf16[1536,256]{1,0:T(8,128)(2,1)} %collective-permute-done.27.refs_2_, ...), custom_call_target="tpu_custom_call" | custom-call | flops 6442450944 | bytes 16777216 | tf_op jit(solution)/shard_map/project/pallas_call | solution.py:245
  336.6 3.1 collective-permute-start.56
  339.9 8.5 %collective-permute-done.54 = bf16[384,512]{1,0:T(8,128)(2,1)S(1)} collective-permute-done((bf16[384,512]{1,0:T(8,128)(2,1)}, bf16[384,512]{1,0:T(8,128)(2,1)S(1)}, u32[]{:S(2)}, u32[]{:S(2)}) %collective-permute-start.54) | collective-permute-done | bytes 393248 | tf_op jit(solution)/shard_map/ppermute | solution.py:285
  348.4 7.0 %collective-permute-done.55 = bf16[384,512]{1,0:T(8,128)(2,1)S(1)} collective-permute-done((bf16[384,512]{1,0:T(8,128)(2,1)}, bf16[384,512]{1,0:T(8,128)(2,1)S(1)}, u32[]{:S(2)}, u32[]{:S(2)}) %collective-permute-start.55) | collective-permute-done | bytes 393248 | tf_op jit(solution)/shard_map/ppermute | solution.py:285
  (244 shorter events, 80.2 us)
Async XLA Ops:
  49.9 44.1 %collective-permute-start.13 = (bf16[1152,256]{1,0:T(8,128)(2,1)S(1)}, bf16[1152,256]{1,0:T(8,128)(2,1)S(1)}, u32[]{:S(2)}, u32[]{:S(2)}) collective-permute-start(bf16[1152,256]{1,0:T(8,128)(2,1)S(1)} %constant_dynamic-update-slice_fusion.refs_12_), channel_id=1, source_target_pairs={{0,2},{2,0},{4,6},{6,4},{1,3},{3,1},{5,7},{7,5},{8,10},{10,8},{12,... | collective-permute-start | bytes 1769480 | tf_op jit(solution)/shard_map/ppermute | solution.py:285
  52.4 41.7 %collective-permute-start.14 = (bf16[1152,256]{1,0:T(8,128)(2,1)S(1)}, bf16[1152,256]{1,0:T(8,128)(2,1)S(1)}, u32[]{:S(2)}, u32[]{:S(2)}) collective-permute-start(bf16[1152,256]{1,0:T(8,128)(2,1)S(1)} %constant_dynamic-update-slice_fusion.refs_12_), channel_id=1, source_target_pairs={{0,4},{2,6},{4,0},{6,2},{1,5},{3,7},{5,1},{7,3},{8,12},{10,14},{12... | collective-permute-start | bytes 1769480 | tf_op jit(solution)/shard_map/ppermute | solution.py:285
  60.8 33.8 %collective-permute-start.15 = (bf16[1152,256]{1,0:T(8,128)(2,1)S(1)}, bf16[1152,256]{1,0:T(8,128)(2,1)S(1)}, u32[]{:S(2)}, u32[]{:S(2)}) collective-permute-start(bf16[1152,256]{1,0:T(8,128)(2,1)S(1)} %constant_dynamic-update-slice_fusion.refs_12_), channel_id=1, source_target_pairs={{0,6},{2,4},{4,2},{6,0},{1,7},{3,5},{5,3},{7,1},{8,14},{10,12},{12... | collective-permute-start | bytes 1769480 | tf_op jit(solution)/shard_map/ppermute | solution.py:285
  60.9 32.5 %collective-permute-start.1 = (bf16[384,512]{1,0:T(8,128)(2,1)}, bf16[384,512]{1,0:T(8,128)(2,1)S(1)}, u32[]{:S(2)}, u32[]{:S(2)}) collective-permute-start(bf16[384,512]{1,0:T(8,128)(2,1)} %get-tuple-element.37), channel_id=1, source_target_pairs={{0,4},{2,6},{4,0},{6,2},{1,5},{3,7},{5,1},{7,3},{8,12},{10,14},{12... | collective-permute-start | bytes 1179656 | tf_op jit(solution)/shard_map/ppermute | solution.py:285
  100.0 37.7 %collective-permute-start.57 = (bf16[256,384]{1,0:T(8,128)(2,1)}, bf16[256,384]{1,0:T(8,128)(2,1)S(1)}, u32[]{:S(2)}, u32[]{:S(2)}) collective-permute-start(bf16[256,384]{1,0:T(8,128)(2,1)} %get-tuple-element.53), channel_id=1, source_target_pairs={{0,2},{2,0},{4,6},{6,4},{1,3},{3,1},{5,7},{7,5},{8,10},{10,8},{12,... | collective-permute-start | bytes 589832 | tf_op jit(solution)/shard_map/ppermute | solution.py:285
  101.4 36.6 %collective-permute-start.58 = (bf16[256,384]{1,0:T(8,128)(2,1)}, bf16[256,384]{1,0:T(8,128)(2,1)S(1)}, u32[]{:S(2)}, u32[]{:S(2)}) collective-permute-start(bf16[256,384]{1,0:T(8,128)(2,1)} %get-tuple-element.54), channel_id=1, source_target_pairs={{0,4},{2,6},{4,0},{6,2},{1,5},{3,7},{5,1},{7,3},{8,12},{10,14},{12... | collective-permute-start | bytes 589832 | tf_op jit(solution)/shard_map/ppermute | solution.py:285
  102.4 36.9 %collective-permute-start.59 = (bf16[256,384]{1,0:T(8,128)(2,1)}, bf16[256,384]{1,0:T(8,128)(2,1)S(1)}, u32[]{:S(2)}, u32[]{:S(2)}) collective-permute-start(bf16[256,384]{1,0:T(8,128)(2,1)} %get-tuple-element.55), channel_id=1, source_target_pairs={{0,6},{2,4},{4,2},{6,0},{1,7},{3,5},{5,3},{7,1},{8,14},{10,12},{12... | collective-permute-start | bytes 589832 | tf_op jit(solution)/shard_map/ppermute | solution.py:285
  103.5 48.6 %collective-permute-start.51 = (bf16[1024,512]{1,0:T(8,128)(2,1)S(1)}, bf16[1024,512]{1,0:T(8,128)(2,1)}, u32[]{:S(2)}, u32[]{:S(2)}) collective-permute-start(bf16[1024,512]{1,0:T(8,128)(2,1)S(1)} %constant_dynamic-update-slice_fusion.3.refs_24_), channel_id=1, source_target_pairs={{0,16},{8,24},{16,0},{24,8},{1,17},{9,25},{17,1},{25,9},{2,18},{10... | collective-permute-start | bytes 3145736 | tf_op jit(solution)/shard_map/ppermute | solution.py:301
  115.6 37.2 %collective-permute-start.34 = (bf16[1536,128]{1,0:T(8,128)(2,1)}, bf16[1536,128]{1,0:T(8,128)(2,1)S(1)}, u32[]{:S(2)}, u32[]{:S(2)}) collective-permute-start(bf16[1536,128]{1,0:T(8,128)(2,1)} %attention.5.refs_9_), channel_id=1, source_target_pairs={{0,2},{2,0},{4,6},{6,4},{1,3},{3,1},{5,7},{7,5},{8,10},{10,8},{12,... | collective-permute-start | bytes 1179656 | tf_op jit(solution)/shard_map/ppermute | solution.py:285
  138.0 51.0 %collective-permute-start.38 = (bf16[1536,128]{1,0:T(8,128)(2,1)S(1)}, bf16[1536,128]{1,0:T(8,128)(2,1)S(1)}, u32[]{:S(2)}, u32[]{:S(2)}) collective-permute-start(bf16[1536,128]{1,0:T(8,128)(2,1)S(1)} %copy-done.25), channel_id=1, source_target_pairs={{0,6},{2,4},{4,2},{6,0},{1,7},{3,5},{5,3},{7,1},{8,14},{10,12},{12... | collective-permute-start | bytes 1179656 | tf_op jit(solution)/shard_map/ppermute | solution.py:285
  139.3 65.8 %collective-permute-start.33 = (bf16[1536,128]{1,0:T(8,128)(2,1)}, bf16[1536,128]{1,0:T(8,128)(2,1)S(1)}, u32[]{:S(2)}, u32[]{:S(2)}) collective-permute-start(bf16[1536,128]{1,0:T(8,128)(2,1)} %attention.4.refs_8_), channel_id=1, source_target_pairs={{0,2},{2,0},{4,6},{6,4},{1,3},{3,1},{5,7},{7,5},{8,10},{10,8},{12,... | collective-permute-start | bytes 1179656 | tf_op jit(solution)/shard_map/ppermute | solution.py:285
  152.1 53.7 %collective-permute-start.35 = (bf16[1536,128]{1,0:T(8,128)(2,1)}, bf16[1536,128]{1,0:T(8,128)(2,1)S(1)}, u32[]{:S(2)}, u32[]{:S(2)}) collective-permute-start(bf16[1536,128]{1,0:T(8,128)(2,1)} %attention.4.refs_8_), channel_id=1, source_target_pairs={{0,4},{2,6},{4,0},{6,2},{1,5},{3,7},{5,1},{7,3},{8,12},{10,14},{12... | collective-permute-start | bytes 1179656 | tf_op jit(solution)/shard_map/ppermute | solution.py:285
  152.8 53.2 %collective-permute-start.37 = (bf16[1536,128]{1,0:T(8,128)(2,1)}, bf16[1536,128]{1,0:T(8,128)(2,1)S(1)}, u32[]{:S(2)}, u32[]{:S(2)}) collective-permute-start(bf16[1536,128]{1,0:T(8,128)(2,1)} %attention.4.refs_8_), channel_id=1, source_target_pairs={{0,6},{2,4},{4,2},{6,0},{1,7},{3,5},{5,3},{7,1},{8,14},{10,12},{12... | collective-permute-start | bytes 1179656 | tf_op jit(solution)/shard_map/ppermute | solution.py:285
  158.8 61.0 %collective-permute-start.61 = (bf16[1024,384]{1,0:T(8,128)(2,1)S(1)}, bf16[1024,384]{1,0:T(8,128)(2,1)S(1)}, u32[]{:S(2)}, u32[]{:S(2)}) collective-permute-start(bf16[1024,384]{1,0:T(8,128)(2,1)S(1)} %constant_dynamic-update-slice_fusion.7.refs_24_), channel_id=1, source_target_pairs={{0,16},{8,24},{16,0},{24,8},{1,17},{9,25},{17,1},{25,9},{2,18},{10... | collective-permute-start | bytes 2359304 | tf_op jit(solution)/shard_map/ppermute | solution.py:301
  221.6 36.5 %collective-permute-start.27 = (bf16[1536,256]{1,0:T(8,128)(2,1)S(1)}, bf16[1536,256]{1,0:T(8,128)(2,1)}, u32[]{:S(2)}, u32[]{:S(2)}) collective-permute-start(bf16[1536,256]{1,0:T(8,128)(2,1)S(1)} %copy-done.10), channel_id=1, source_target_pairs={{0,4},{2,6},{4,0},{6,2},{1,5},{3,7},{5,1},{7,3},{8,12},{10,14},{12... | collective-permute-start | bytes 2359304 | tf_op jit(solution)/shard_map/ppermute | solution.py:285
  222.2 36.0 %collective-permute-start.28 = (bf16[1536,256]{1,0:T(8,128)(2,1)S(1)}, bf16[1536,256]{1,0:T(8,128)(2,1)}, u32[]{:S(2)}, u32[]{:S(2)}) collective-permute-start(bf16[1536,256]{1,0:T(8,128)(2,1)S(1)} %copy-done.10), channel_id=1, source_target_pairs={{0,6},{2,4},{4,2},{6,0},{1,7},{3,5},{5,3},{7,1},{8,14},{10,12},{12... | collective-permute-start | bytes 2359304 | tf_op jit(solution)/shard_map/ppermute | solution.py:285
  225.1 33.6 %collective-permute-start.29 = (bf16[1536,256]{1,0:T(8,128)(2,1)S(1)}, bf16[1536,256]{1,0:T(8,128)(2,1)S(1)}, u32[]{:S(2)}, u32[]{:S(2)}) collective-permute-start(bf16[1536,256]{1,0:T(8,128)(2,1)S(1)} %copy-done.10), channel_id=1, source_target_pairs={{1,0},{0,1},{3,2},{2,3},{5,4},{4,5},{7,6},{6,7},{9,8},{8,9},{11,10... | collective-permute-start | bytes 2359304 | tf_op jit(solution)/shard_map/ppermute | solution.py:297
  225.2 50.1 %collective-permute-start.63 = (bf16[1024,384]{1,0:T(8,128)(2,1)S(1)}, bf16[1024,384]{1,0:T(8,128)(2,1)S(1)}, u32[]{:S(2)}, u32[]{:S(2)}) collective-permute-start(bf16[1024,384]{1,0:T(8,128)(2,1)S(1)} %collective-permute-done.61.refs_26_), channel_id=1, source_target_pairs={{8,0},{16,24},{9,1},{17,25},{10,2},{18,26},{11,3},{19,27},{12,4},{... | collective-permute-start | bytes 2359304 | tf_op jit(solution)/shard_map/ppermute | solution.py:301
  238.1 38.9 %collective-permute-start.30 = (bf16[1536,256]{1,0:T(8,128)(2,1)S(1)}, bf16[1536,256]{1,0:T(8,128)(2,1)S(1)}, u32[]{:S(2)}, u32[]{:S(2)}) collective-permute-start(bf16[1536,256]{1,0:T(8,128)(2,1)S(1)} %collective-permute-done.26.refs_1_), channel_id=1, source_target_pairs={{1,0},{0,1},{3,2},{2,3},{5,4},{4,5},{7,6},{6,7},{9,8},{8,9},{11,10... | collective-permute-start | bytes 2359304 | tf_op jit(solution)/shard_map/ppermute | solution.py:297
  258.7 40.6 %collective-permute-start.50 = (bf16[1024,512]{1,0:T(8,128)(2,1)S(1)}, bf16[1024,512]{1,0:T(8,128)(2,1)S(1)}, u32[]{:S(2)}, u32[]{:S(2)}) collective-permute-start(bf16[1024,512]{1,0:T(8,128)(2,1)S(1)} %constant_dynamic-update-slice_fusion.3.refs_24_), channel_id=1, source_target_pairs={{0,8},{8,0},{16,24},{24,16},{1,9},{9,1},{17,25},{25,17},{2,10},{10... | collective-permute-start | bytes 3145736 | tf_op jit(solution)/shard_map/ppermute | solution.py:301
  277.9 43.3 %collective-permute-start.53 = (bf16[1024,512]{1,0:T(8,128)(2,1)}, bf16[1024,512]{1,0:T(8,128)(2,1)}, u32[]{:S(2)}, u32[]{:S(2)}) collective-permute-start(bf16[1024,512]{1,0:T(8,128)(2,1)} %collective-permute-done.51.refs_26_), channel_id=1, source_target_pairs={{8,0},{16,24},{9,1},{17,25},{10,2},{18,26},{11,3},{19,27},{12,4},{... | collective-permute-start | bytes 3145736 | tf_op jit(solution)/shard_map/ppermute | solution.py:301
  294.7 41.9 %collective-permute-start.64 = (bf16[384,384]{1,0:T(8,128)(2,1)}, bf16[384,384]{1,0:T(8,128)(2,1)S(1)}, u32[]{:S(2)}, u32[]{:S(2)}) collective-permute-start(bf16[384,384]{1,0:T(8,128)(2,1)} %get-tuple-element.62), channel_id=1, source_target_pairs={{0,2},{2,0},{4,6},{6,4},{1,3},{3,1},{5,7},{7,5},{8,10},{10,8},{12,... | collective-permute-start | bytes 884744 | tf_op jit(solution)/shard_map/ppermute | solution.py:285
  294.8 44.9 %collective-permute-start.65 = (bf16[384,384]{1,0:T(8,128)(2,1)}, bf16[384,384]{1,0:T(8,128)(2,1)S(1)}, u32[]{:S(2)}, u32[]{:S(2)}) collective-permute-start(bf16[384,384]{1,0:T(8,128)(2,1)} %get-tuple-element.63), channel_id=1, source_target_pairs={{0,4},{2,6},{4,0},{6,2},{1,5},{3,7},{5,1},{7,3},{8,12},{10,14},{12... | collective-permute-start | bytes 884744 | tf_op jit(solution)/shard_map/ppermute | solution.py:285
  300.2 39.5 %collective-permute-start.66 = (bf16[384,384]{1,0:T(8,128)(2,1)}, bf16[384,384]{1,0:T(8,128)(2,1)S(1)}, u32[]{:S(2)}, u32[]{:S(2)}) collective-permute-start(bf16[384,384]{1,0:T(8,128)(2,1)} %get-tuple-element.64), channel_id=1, source_target_pairs={{0,6},{2,4},{4,2},{6,0},{1,7},{3,5},{5,3},{7,1},{8,14},{10,12},{12... | collective-permute-start | bytes 884744 | tf_op jit(solution)/shard_map/ppermute | solution.py:285
  (95 other events, 2371.9 us)

commit v2 on v1

--- a/solution.py
+++ b/solution.py
@@ -67,7 +67,7 @@
     own, refs = refs[: cols * group], refs[cols * group :]
     before, refs = refs[: cols * group], refs[cols * group :]
     w_refs, refs = refs[:planes], refs[planes:]
-    o_ref, q_sc, w_sc, kv_sc, m_sc, acc_sc = refs
+    o_ref, q_sc, w_sc, kv_sc, m_sc, acc_sc, before_sc, sems = refs
     grp, mem, col = place[0], place[1], place[2]
     tok, features = own[0].shape
     plane = tok * group
@@ -77,11 +77,21 @@
     rows = size // parts
     depth = w_refs[0].shape[1]
 
-    def expand(sources, at, to):
+    first_step = jnp.logical_and(pl.program_id(0) == 0, block == 0)
+    copies = [
+        pltpu.make_async_copy(before[i], before_sc.at[i], sems.at[i]) for i in range(cols * group)
+    ]
+
+    @pl.when(first_step)
+    def _():
+        for copy in copies:
+            copy.start()
+
+    def expand(load, to):
         out = None
         for s in range(cols):
             w = w_sc[pl.ds(pl.multiple_of(((col + s) % cols) * features, features), features), :]
-            term = jnp.dot(sources[s * group][at, :], w, preferred_element_type=jnp.float32)
+            term = jnp.dot(load(s), w, preferred_element_type=jnp.float32)
             out = term if out is None else out + term
         kv_sc[to, :] = out.astype(kv_sc.dtype)
 
@@ -94,15 +104,7 @@
                 w_sc[pl.ds(pl.multiple_of(first, depth), depth), :] = w_refs[k][m]
         for m in range(group):
             first = earlier + (mem ^ m) * tok
-            expand(own[m:], pl.ds(0, tok), pl.ds(pl.multiple_of(first, tok), tok))
-
-        def plane_before(t, _):
-            for m in range(group):
-                at = pl.ds(pl.multiple_of(t * tok, tok), tok)
-                expand(before[m:], at, pl.ds(pl.multiple_of(t * plane + m * tok, tok), tok))
-            return 0
-
-        lax.fori_loop(planes - 1 - grp, planes - 1, plane_before, 0)
+            expand(lambda s: own[s * group + m][...], pl.ds(pl.multiple_of(first, tok), tok))
 
     m_sc[...] = jnp.full_like(m_sc, NEG_FILL)
     acc_sc[...] = jnp.zeros_like(acc_sc)
@@ -147,19 +149,37 @@
         def _():
             step(earlier, (b + 1) * size, b * size)
 
+    @pl.when(first_step)
+    def _():
+        for copy in copies:
+            copy.wait()
+
+    @pl.when(block == 0)
+    def _():
+        def plane_before(t, _):
+            at = pl.ds(pl.multiple_of(t * tok, tok), tok)
+            for m in range(group):
+                expand(
+                    lambda s: before_sc[s * group + m, at, :],
+                    pl.ds(pl.multiple_of(t * plane + m * tok, tok), tok),
+                )
+            return 0
+
+        lax.fori_loop(planes - 1 - grp, planes - 1, plane_before, 0)
+
     lax.fori_loop(planes - 1 - grp, planes - 1, plane_step, 0)
     o_ref[...] = (acc_sc[:, :HEAD] / acc_sc[:, HEAD:]).astype(o_ref.dtype)
 
 
-def attention(place, queries, own, before, w, first_head, heads):
+def attention(place, queries, own, before, w, first_query, first_head, heads):
     planes, group, cols = len(w), len(queries), len(own)
     tok, features = own[0][0].shape
     plane = tok * group
     total = planes * plane
-    size = plane // 2
+    size = plane
     fixed = lambda h, j, s: (0, 0)
     whole = [pl.BlockSpec(x.shape, fixed, pipeline_mode=pl.Buffered(1)) for x in own[0] * cols]
-    whole += [pl.BlockSpec(x.shape, fixed, pipeline_mode=pl.Buffered(1)) for x in before[0] * cols]
+    whole += [pl.BlockSpec(memory_space=pl.ANY) for _ in before[0] * cols]
     return pl.pallas_call(
         functools.partial(
             attention_kernel,
@@ -173,7 +193,7 @@
         grid_spec=pltpu.PrefetchScalarGridSpec(
             num_scalar_prefetch=1,
             grid=(heads, plane // size),
-            in_specs=[pl.BlockSpec((tok, HEAD), lambda h, j, s: (0, h + first_head)) for _ in queries]
+            in_specs=[pl.BlockSpec((tok, HEAD), lambda h, j, s: (0, h + first_query)) for _ in queries]
             + whole
             + [
                 pl.BlockSpec((*x.shape[:2], 2 * HEAD), lambda h, j, s: (0, 0, h + first_head)) for x in w
@@ -185,6 +205,8 @@
                 pltpu.VMEM((total, 2 * HEAD), jnp.bfloat16),
                 pltpu.VMEM((size, HEAD), jnp.float32),
                 pltpu.VMEM((size, 2 * HEAD), jnp.float32),
+                pltpu.VMEM((cols * group, *before[0][0].shape), jnp.bfloat16),
+                pltpu.SemaphoreType.DMA((cols * group,)),
             ],
         ),
         compiler_params=pltpu.CompilerParams(
@@ -319,7 +341,7 @@
     takes = [
         by_turn(run * 2 * HEAD),
         [(m, width, [span]) for span in spans for m in shifts],
-        by_turn(run * HEAD),
+        [(m, run * HEAD, [(t * group * run * HEAD, run * HEAD)]) for t in range(turns) for m in shifts],
     ]
     blocks = cut(place, [w_kv, w_out, queries], takes)
     w_mine = exchange(blocks[:group])
@@ -338,7 +360,7 @@
 
     out_first = spread(w_first)
     below = gather(jnp.concatenate(lower))
-    my_queries = exchange(blocks[3 * group :])
+    my_queries = [exchange(blocks[(3 + t) * group : (4 + t) * group]) for t in range(turns)]
     w_second = exchange(blocks[2 * group : 3 * group])
 
     owns = [own] + [[across(x, s) for x in own] for s in range(1, cols)]
@@ -350,12 +372,12 @@
     done = []
     for turn, first_head, heads in calls:
         i = len(done)
-        done.append(attention(place, my_queries, owns, belows, w_all, first_head, heads))
+        done.append(attention(place, my_queries[turn], owns, belows, w_all, first_head - turn * run, first_head, heads))
         results[turn].append(gather(done[-1]))
         if i == 0:
             w_second, _ = lax.optimization_barrier((w_second, done[0]))
             out_second = spread(w_second)
-    middle, _ = lax.optimization_barrier((out_first[1], done[max(len(done) - 2, 0)]))
+    middle, _ = lax.optimization_barrier((out_first[1], done[0]))
     first_far = relay(middle)
     middle, _ = lax.optimization_barrier((out_second[1], done[-1]))
     second_far = relay(middle)

time: 359 us -> 334 us (0.930)
  starting transfers between devices: 130 us -> 109 us
  Pallas kernels: 63.1 us -> 59 us
    ppermute x11, waiting for transfers between devices: 54.4 us -> 76.7 us  [plane_swap(): return lax.ppermute(x, 'grp', [(z, z ^ k) for z in senders])]
    ppermute x11, starting transfers between devices: 74.5 us -> 53.4 us  [plane_swap(): return lax.ppermute(x, 'grp', [(z, z ^ k) for z in senders])]
    ppermute x33 -> x36, waiting for transfers between devices: 93.3 us -> 73.4 us  [swap(): return lax.ppermute(x, 'mem', [(p, p ^ m) for p in range(group)])]
    pallas_call x3, Pallas kernels: 28.3 us -> 24.5 us  [attention(): pl.pallas_call(functools.partial(attention_kernel, planes=planes, group=g...]
    ppermute x33 -> x36, starting transfers between devices: 41.6 us -> 41.1 us  [swap(): return lax.ppermute(x, 'mem', [(p, p ^ m) for p in range(group)])]
  transfers between devices with their start and end apart: 67 -> 70, of which waited for: 24 -> 25; matrix products, arithmetic and copies ran while one was open for 1% -> 1% of each run, Pallas kernels for 16% -> 18%
where the time goes in v2:
time: 334 us
  waiting for transfers between devices  156 us (47%)
  starting transfers between devices  109 us (33%)
  Pallas kernels  59 us (18%)
  local copies, waits for them, and re-layouts  6.79 us (2%)
    ppermute x11, waiting for transfers between devices, plane_swap(): return lax.ppermute(x, 'grp', [(z, z ^ k) for z in senders])  76.7 us
    ppermute x36, waiting for transfers between devices, swap(): return lax.ppermute(x, 'mem', [(p, p ^ m) for p in range(group)])  73.4 us
    ppermute x11, starting transfers between devices, plane_swap(): return lax.ppermute(x, 'grp', [(z, z ^ k) for z in senders])  53.4 us
    ppermute x36, starting transfers between devices, swap(): return lax.ppermute(x, 'mem', [(p, p ^ m) for p in range(group)])  41.1 us
    pallas_call x2, Pallas kernels, project(): pl.pallas_call(functools.partial(project_kernel, counts=[len(some) for so...  29.5 us
    pallas_call x3, Pallas kernels, attention(): pl.pallas_call(functools.partial(attention_kernel, planes=planes, group=g...  24.5 us
    ppermute x3, starting transfers between devices, up(): return lax.ppermute(x, 'grp', [(z, z + k) for z in range(planes - k)])  10.7 us
  transfers between devices with their start and end apart: 70, of which 25 were waited for; matrix products, arithmetic and copies ran while one was open for 1% of the time, Pallas kernels for 18%

profile of v2, /device:TPU:0, one launch (start us, length us, event | category | flops | bytes accessed | tf_op | source)
XLA Modules:
  0.0 333.6 jit_solution(2755966985517802629)
XLA Ops:
  0.0 7.0 %collective-permute-start.10 = (bf16[384,256]{1,0:T(8,128)(2,1)}, bf16[384,256]{1,0:T(8,128)(2,1)S(1)}, u32[]{:S(2)}, u32[]{:S(2)}) collective-permute-start(bf16[384,256]{1,0:T(8,128)(2,1)} %refs_4_.5), channel_id=1, source_target_pairs={{0,24},{1,25},{2,26},{3,27},{4,28},{5,29},{6,30},{7,31}} | collective-permute-start | bytes 589832 | tf_op jit(solution)/shard_map/ppermute | solution.py:316
  9.0 5.0 %cut.1 = (bf16[32,1024]{1,0:T(8,128)(2,1)}, bf16[32,1024]{1,0:T(8,128)(2,1)}, bf16[32,1024]{1,0:T(8,128)(2,1)}, bf16[32,1024]{1,0:T(8,128)(2,1)}, bf16[256,512]{...) custom-call(s32[3]{0:T(128)} %pad_add_fusion.place, ...), custom_call_target="tpu_custom_call" | custom-call | bytes 7340032 | tf_op jit(solution)/shard_map/cut/pallas_call | solution.py:42
  20.1 3.4 %collective-permute-done.22 = bf16[32,1024]{1,0:T(8,128)(2,1)S(1)} collective-permute-done((bf16[32,1024]{1,0:T(8,128)(2,1)}, bf16[32,1024]{1,0:T(8,128)(2,1)S(1)}, u32[]{:S(2)}, u32[]{:S(2)}) %collective-permute-start.22) | collective-permute-done | bytes 65568 | tf_op jit(solution)/shard_map/ppermute | solution.py:307
  37.8 6.9 %collective-permute-done.33.refs_1_ = bf16[384,256]{1,0:T(8,128)(2,1)S(1)} collective-permute-done((bf16[384,256]{1,0:T(8,128)(2,1)}, bf16[384,256]{1,0:T(8,128)(2,1)S(1)}, u32[]{:S(2)}, u32[]{:S(2)}) %collective-permute-start.33) | collective-permute-done | bytes 196640 | tf_op jit(solution)/shard_map/ppermute | solution.py:307
  55.1 10.2 %collective-permute-done.23.refs_21_ = bf16[4,32,1024]{2,1,0:T(8,128)(2,1)S(1)} collective-permute-done((bf16[4,32,1024]{2,1,0:T(8,128)(2,1)S(1)}, bf16[4,32,1024]{2,1,0:T(8,128)(2,1)S(1)}, u32[]{:S(2)}, u32[]{:S(2)}) %collective-permute-start.23) | collective-permute-done | bytes 262176 | tf_op jit(solution)/shard_map/ppermute | solution.py:323
  65.5 4.8 %collective-permute-done.24.refs_22_ = bf16[4,32,1024]{2,1,0:T(8,128)(2,1)S(1)} collective-permute-done((bf16[4,32,1024]{2,1,0:T(8,128)(2,1)S(1)}, bf16[4,32,1024]{2,1,0:T(8,128)(2,1)S(1)}, u32[]{:S(2)}, u32[]{:S(2)}) %collective-permute-start.24) | collective-permute-done | bytes 262176 | tf_op jit(solution)/shard_map/ppermute | solution.py:323
  70.3 3.2 collective-permute-done.25.refs_23_
  74.0 4.9 %collective-permute-done.14.refs_14_ = bf16[1152,256]{1,0:T(8,128)(2,1)S(1)} collective-permute-done((bf16[1152,256]{1,0:T(8,128)(2,1)S(1)}, bf16[1152,256]{1,0:T(8,128)(2,1)S(1)}, u32[]{:S(2)}, u32[]{:S(2)}) %collective-permute-start.14) | collective-permute-done | bytes 589856 | tf_op jit(solution)/shard_map/ppermute | solution.py:307
  89.5 7.0 %attention.5.refs_9_ = bf16[1536,128]{1,0:T(8,128)(2,1)} custom-call(s32[3]{0:T(128)} %pad_add_fusion.place, bf16[384,256]{1,0:T(8,128)(2,1)} %get-tuple-element.47.refs_0_, bf16[384,256]{1,0:T(8,128)(2,1)} %copy-done.51, bf16[384,256]{1,0:T(8,128)(2,1)} %copy-done.52, bf16[384,256]{1,0:T(8,128)(2,1)} %copy-done.53, bf16[384,256]{1,0:T(8,128)(2,1)} %refs_4_.5, ...), custom_call_target="tpu_custom_call" | custom-call | flops 7247757312 | bytes 6291456 | tf_op jit(solution)/shard_map/attention/pallas_call | solution.py:183
  97.9 6.5 %collective-permute-start.54 = (bf16[1024,512]{1,0:T(8,128)(2,1)S(1)}, bf16[1024,512]{1,0:T(8,128)(2,1)}, u32[]{:S(2)}, u32[]{:S(2)}) collective-permute-start(bf16[1024,512]{1,0:T(8,128)(2,1)S(1)} %constant_dynamic-update-slice_fusion.3.refs_24_), channel_id=1, source_target_pairs={{0,16},{8,24},{16,0},{24,8},{1,17},{9,25},{17,1},{25,9},{2,18},{10... | collective-permute-start | bytes 3145736 | tf_op jit(solution)/shard_map/ppermute | solution.py:323
  105.5 10.5 %attention.3.refs_0_ = bf16[1536,256]{1,0:T(8,128)(2,1)} custom-call(s32[3]{0:T(128)} %pad_add_fusion.place, bf16[384,256]{1,0:T(8,128)(2,1)} %get-tuple-element.39.refs_0_, bf16[384,256]{1,0:T(8,128)(2,1)} %collective-permute-done.refs_1_, bf16[384,256]{1,0:T(8,128)(2,1)} %collective-permute-done.1.refs_2_, ...), custom_call_target="tpu_custom_call" | custom-call | flops 14495514624 | bytes 6291456 | tf_op jit(solution)/shard_map/attention/pallas_call | solution.py:183
  116.0 7.1 %attention.4.refs_8_ = bf16[1536,128]{1,0:T(8,128)(2,1)} custom-call(s32[3]{0:T(128)} %pad_add_fusion.place, bf16[384,256]{1,0:T(8,128)(2,1)} %get-tuple-element.47.refs_0_, bf16[384,256]{1,0:T(8,128)(2,1)} %copy-done.51, bf16[384,256]{1,0:T(8,128)(2,1)} %copy-done.52, bf16[384,256]{1,0:T(8,128)(2,1)} %copy-done.53, bf16[384,256]{1,0:T(8,128)(2,1)} %refs_4_.5, ...), custom_call_target="tpu_custom_call" | custom-call | flops 7247757312 | bytes 6291456 | tf_op jit(solution)/shard_map/attention/pallas_call | solution.py:183
  126.9 21.9 %collective-permute-done.54.refs_26_ = bf16[1024,512]{1,0:T(8,128)(2,1)} collective-permute-done((bf16[1024,512]{1,0:T(8,128)(2,1)S(1)}, bf16[1024,512]{1,0:T(8,128)(2,1)}, u32[]{:S(2)}, u32[]{:S(2)}) %collective-permute-start.54) | collective-permute-done | bytes 1048608 | tf_op jit(solution)/shard_map/ppermute | solution.py:323
  151.4 14.8 %collective-permute-start.64 = (bf16[1024,384]{1,0:T(8,128)(2,1)S(1)}, bf16[1024,384]{1,0:T(8,128)(2,1)S(1)}, u32[]{:S(2)}, u32[]{:S(2)}) collective-permute-start(bf16[1024,384]{1,0:T(8,128)(2,1)S(1)} %constant_dynamic-update-slice_fusion.7.refs_24_), channel_id=1, source_target_pairs={{0,16},{8,24},{16,0},{24,8},{1,17},{9,25},{17,1},{25,9},{2,18},{10... | collective-permute-start | bytes 2359304 | tf_op jit(solution)/shard_map/ppermute | solution.py:323
  166.2 13.5 %collective-permute-start.63 = (bf16[1024,384]{1,0:T(8,128)(2,1)S(1)}, bf16[1024,384]{1,0:T(8,128)(2,1)S(1)}, u32[]{:S(2)}, u32[]{:S(2)}) collective-permute-start(bf16[1024,384]{1,0:T(8,128)(2,1)S(1)} %constant_dynamic-update-slice_fusion.7.refs_24_), channel_id=1, source_target_pairs={{0,8},{8,0},{16,24},{24,16},{1,9},{9,1},{17,25},{25,17},{2,10},{10... | collective-permute-start | bytes 2359304 | tf_op jit(solution)/shard_map/ppermute | solution.py:323
  183.6 14.1 %collective-permute-done.64.refs_26_ = bf16[1024,384]{1,0:T(8,128)(2,1)S(1)} collective-permute-done((bf16[1024,384]{1,0:T(8,128)(2,1)S(1)}, bf16[1024,384]{1,0:T(8,128)(2,1)S(1)}, u32[]{:S(2)}, u32[]{:S(2)}) %collective-permute-start.64) | collective-permute-done | bytes 786464 | tf_op jit(solution)/shard_map/ppermute | solution.py:323
  204.4 10.8 %collective-permute-done.26.refs_1_ = bf16[1536,256]{1,0:T(8,128)(2,1)S(1)} collective-permute-done((bf16[1536,256]{1,0:T(8,128)(2,1)S(1)}, bf16[1536,256]{1,0:T(8,128)(2,1)S(1)}, u32[]{:S(2)}, u32[]{:S(2)}) %collective-permute-start.26) | collective-permute-done | bytes 786464 | tf_op jit(solution)/shard_map/ppermute | solution.py:307
  215.2 21.7 %collective-permute-done.27.refs_2_ = bf16[1536,256]{1,0:T(8,128)(2,1)} collective-permute-done((bf16[1536,256]{1,0:T(8,128)(2,1)S(1)}, bf16[1536,256]{1,0:T(8,128)(2,1)}, u32[]{:S(2)}, u32[]{:S(2)}) %collective-permute-start.27) | collective-permute-done | bytes 786464 | tf_op jit(solution)/shard_map/ppermute | solution.py:307
  237.4 12.6 %collective-permute-start.53 = (bf16[1024,512]{1,0:T(8,128)(2,1)S(1)}, bf16[1024,512]{1,0:T(8,128)(2,1)S(1)}, u32[]{:S(2)}, u32[]{:S(2)}) collective-permute-start(bf16[1024,512]{1,0:T(8,128)(2,1)S(1)} %constant_dynamic-update-slice_fusion.3.refs_24_), channel_id=1, source_target_pairs={{0,8},{8,0},{16,24},{24,16},{1,9},{9,1},{17,25},{25,17},{2,10},{10... | collective-permute-start | bytes 3145736 | tf_op jit(solution)/shard_map/ppermute | solution.py:323
  254.6 14.5 %project.3 = (bf16[384,384]{1,0:T(8,128)(2,1)}, bf16[384,384]{1,0:T(8,128)(2,1)}, bf16[384,384]{1,0:T(8,128)(2,1)}, bf16[384,384]{1,0:T(8,128)(2,1)}) custom-call(s32[6]{0:T(128)} %stack.86.scalars, bf16[1536,256]{1,0:T(8,128)(2,1)} %attention.3.refs_0_, bf16[1536,256]{1,0:T(8,128)(2,1)} %copy-done.12, bf16[1536,256]{1,0:T(8,128)(2,1)} %collective-permute-done.27.refs_2_, ...), custom_call_target="tpu_custom_call" | custom-call | flops 4831838208 | bytes 15728640 | tf_op jit(solution)/shard_map/project/pallas_call | solution.py:267
  276.3 19.6 %collective-permute-done.56.refs_28_ = bf16[1024,512]{1,0:T(8,128)(2,1)} collective-permute-done((bf16[1024,512]{1,0:T(8,128)(2,1)}, bf16[1024,512]{1,0:T(8,128)(2,1)}, u32[]{:S(2)}, u32[]{:S(2)}) %collective-permute-start.56) | collective-permute-done | bytes 1048608 | tf_op jit(solution)/shard_map/ppermute | solution.py:323
  295.9 14.9 %project.2 = (bf16[384,512]{1,0:T(8,128)(2,1)}, bf16[384,512]{1,0:T(8,128)(2,1)}, bf16[384,512]{1,0:T(8,128)(2,1)}, bf16[384,512]{1,0:T(8,128)(2,1)}) custom-call(s32[6]{0:T(128)} %stack.86.scalars, bf16[1536,256]{1,0:T(8,128)(2,1)} %attention.3.refs_0_, bf16[1536,256]{1,0:T(8,128)(2,1)} %copy-done.12, bf16[1536,256]{1,0:T(8,128)(2,1)} %collective-permute-done.27.refs_2_, ...), custom_call_target="tpu_custom_call" | custom-call | flops 6442450944 | bytes 16777216 | tf_op jit(solution)/shard_map/project/pallas_call | solution.py:267
  314.6 8.5 %collective-permute-done.57 = bf16[384,512]{1,0:T(8,128)(2,1)S(1)} collective-permute-done((bf16[384,512]{1,0:T(8,128)(2,1)}, bf16[384,512]{1,0:T(8,128)(2,1)S(1)}, u32[]{:S(2)}, u32[]{:S(2)}) %collective-permute-start.57) | collective-permute-done | bytes 393248 | tf_op jit(solution)/shard_map/ppermute | solution.py:307
  323.1 7.6 %collective-permute-done.58 = bf16[384,512]{1,0:T(8,128)(2,1)S(1)} collective-permute-done((bf16[384,512]{1,0:T(8,128)(2,1)}, bf16[384,512]{1,0:T(8,128)(2,1)S(1)}, u32[]{:S(2)}, u32[]{:S(2)}) %collective-permute-start.58) | collective-permute-done | bytes 393248 | tf_op jit(solution)/shard_map/ppermute | solution.py:307
  (260 shorter events, 81.8 us)
Async XLA Ops:
  49.3 29.6 %collective-permute-start.14 = (bf16[1152,256]{1,0:T(8,128)(2,1)S(1)}, bf16[1152,256]{1,0:T(8,128)(2,1)S(1)}, u32[]{:S(2)}, u32[]{:S(2)}) collective-permute-start(bf16[1152,256]{1,0:T(8,128)(2,1)S(1)} %constant_dynamic-update-slice_fusion.refs_12_), channel_id=1, source_target_pairs={{0,4},{2,6},{4,0},{6,2},{1,5},{3,7},{5,1},{7,3},{8,12},{10,14},{12... | collective-permute-start | bytes 1769480 | tf_op jit(solution)/shard_map/ppermute | solution.py:307
  50.5 28.3 %collective-permute-start.15 = (bf16[1152,256]{1,0:T(8,128)(2,1)S(1)}, bf16[1152,256]{1,0:T(8,128)(2,1)S(1)}, u32[]{:S(2)}, u32[]{:S(2)}) collective-permute-start(bf16[1152,256]{1,0:T(8,128)(2,1)S(1)} %constant_dynamic-update-slice_fusion.refs_12_), channel_id=1, source_target_pairs={{0,6},{2,4},{4,2},{6,0},{1,7},{3,5},{5,3},{7,1},{8,14},{10,12},{12... | collective-permute-start | bytes 1769480 | tf_op jit(solution)/shard_map/ppermute | solution.py:307
  87.1 36.0 %collective-permute-start.60 = (bf16[256,384]{1,0:T(8,128)(2,1)}, bf16[256,384]{1,0:T(8,128)(2,1)S(1)}, u32[]{:S(2)}, u32[]{:S(2)}) collective-permute-start(bf16[256,384]{1,0:T(8,128)(2,1)} %get-tuple-element.61), channel_id=1, source_target_pairs={{0,2},{2,0},{4,6},{6,4},{1,3},{3,1},{5,7},{7,5},{8,10},{10,8},{12,... | collective-permute-start | bytes 589832 | tf_op jit(solution)/shard_map/ppermute | solution.py:307
  88.5 35.7 %collective-permute-start.61 = (bf16[256,384]{1,0:T(8,128)(2,1)}, bf16[256,384]{1,0:T(8,128)(2,1)S(1)}, u32[]{:S(2)}, u32[]{:S(2)}) collective-permute-start(bf16[256,384]{1,0:T(8,128)(2,1)} %get-tuple-element.62), channel_id=1, source_target_pairs={{0,4},{2,6},{4,0},{6,2},{1,5},{3,7},{5,1},{7,3},{8,12},{10,14},{12... | collective-permute-start | bytes 589832 | tf_op jit(solution)/shard_map/ppermute | solution.py:307
  96.5 29.1 %collective-permute-start.62 = (bf16[256,384]{1,0:T(8,128)(2,1)S(1)}, bf16[256,384]{1,0:T(8,128)(2,1)S(1)}, u32[]{:S(2)}, u32[]{:S(2)}) collective-permute-start(bf16[256,384]{1,0:T(8,128)(2,1)S(1)} %copy-done.43), channel_id=1, source_target_pairs={{0,6},{2,4},{4,2},{6,0},{1,7},{3,5},{5,3},{7,1},{8,14},{10,12},{12... | collective-permute-start | bytes 589832 | tf_op jit(solution)/shard_map/ppermute | solution.py:307
  97.9 50.9 %collective-permute-start.54 = (bf16[1024,512]{1,0:T(8,128)(2,1)S(1)}, bf16[1024,512]{1,0:T(8,128)(2,1)}, u32[]{:S(2)}, u32[]{:S(2)}) collective-permute-start(bf16[1024,512]{1,0:T(8,128)(2,1)S(1)} %constant_dynamic-update-slice_fusion.3.refs_24_), channel_id=1, source_target_pairs={{0,16},{8,24},{16,0},{24,8},{1,17},{9,25},{17,1},{25,9},{2,18},{10... | collective-permute-start | bytes 3145736 | tf_op jit(solution)/shard_map/ppermute | solution.py:323
  104.4 45.3 %collective-permute-start.37 = (bf16[1536,128]{1,0:T(8,128)(2,1)}, bf16[1536,128]{1,0:T(8,128)(2,1)S(1)}, u32[]{:S(2)}, u32[]{:S(2)}) collective-permute-start(bf16[1536,128]{1,0:T(8,128)(2,1)} %attention.5.refs_9_), channel_id=1, source_target_pairs={{0,2},{2,0},{4,6},{6,4},{1,3},{3,1},{5,7},{7,5},{8,10},{10,8},{12,... | collective-permute-start | bytes 1179656 | tf_op jit(solution)/shard_map/ppermute | solution.py:307
  123.1 28.3 %collective-permute-start.39 = (bf16[1536,128]{1,0:T(8,128)(2,1)S(1)}, bf16[1536,128]{1,0:T(8,128)(2,1)S(1)}, u32[]{:S(2)}, u32[]{:S(2)}) collective-permute-start(bf16[1536,128]{1,0:T(8,128)(2,1)S(1)} %copy-done.25), channel_id=1, source_target_pairs={{0,4},{2,6},{4,0},{6,2},{1,5},{3,7},{5,1},{7,3},{8,12},{10,14},{12... | collective-permute-start | bytes 1179656 | tf_op jit(solution)/shard_map/ppermute | solution.py:307
  124.2 42.0 %collective-permute-start.41 = (bf16[1536,128]{1,0:T(8,128)(2,1)S(1)}, bf16[1536,128]{1,0:T(8,128)(2,1)S(1)}, u32[]{:S(2)}, u32[]{:S(2)}) collective-permute-start(bf16[1536,128]{1,0:T(8,128)(2,1)S(1)} %copy-done.25), channel_id=1, source_target_pairs={{0,6},{2,4},{4,2},{6,0},{1,7},{3,5},{5,3},{7,1},{8,14},{10,12},{12... | collective-permute-start | bytes 1179656 | tf_op jit(solution)/shard_map/ppermute | solution.py:307
  125.6 54.1 %collective-permute-start.36 = (bf16[1536,128]{1,0:T(8,128)(2,1)}, bf16[1536,128]{1,0:T(8,128)(2,1)S(1)}, u32[]{:S(2)}, u32[]{:S(2)}) collective-permute-start(bf16[1536,128]{1,0:T(8,128)(2,1)} %attention.4.refs_8_), channel_id=1, source_target_pairs={{0,2},{2,0},{4,6},{6,4},{1,3},{3,1},{5,7},{7,5},{8,10},{10,8},{12,... | collective-permute-start | bytes 1179656 | tf_op jit(solution)/shard_map/ppermute | solution.py:307
  148.8 31.7 %collective-permute-start.38 = (bf16[1536,128]{1,0:T(8,128)(2,1)}, bf16[1536,128]{1,0:T(8,128)(2,1)S(1)}, u32[]{:S(2)}, u32[]{:S(2)}) collective-permute-start(bf16[1536,128]{1,0:T(8,128)(2,1)} %attention.4.refs_8_), channel_id=1, source_target_pairs={{0,4},{2,6},{4,0},{6,2},{1,5},{3,7},{5,1},{7,3},{8,12},{10,14},{12... | collective-permute-start | bytes 1179656 | tf_op jit(solution)/shard_map/ppermute | solution.py:307
  149.7 30.8 %collective-permute-start.40 = (bf16[1536,128]{1,0:T(8,128)(2,1)}, bf16[1536,128]{1,0:T(8,128)(2,1)S(1)}, u32[]{:S(2)}, u32[]{:S(2)}) collective-permute-start(bf16[1536,128]{1,0:T(8,128)(2,1)} %attention.4.refs_8_), channel_id=1, source_target_pairs={{0,6},{2,4},{4,2},{6,0},{1,7},{3,5},{5,3},{7,1},{8,14},{10,12},{12... | collective-permute-start | bytes 1179656 | tf_op jit(solution)/shard_map/ppermute | solution.py:307
  151.4 46.3 %collective-permute-start.64 = (bf16[1024,384]{1,0:T(8,128)(2,1)S(1)}, bf16[1024,384]{1,0:T(8,128)(2,1)S(1)}, u32[]{:S(2)}, u32[]{:S(2)}) collective-permute-start(bf16[1024,384]{1,0:T(8,128)(2,1)S(1)} %constant_dynamic-update-slice_fusion.7.refs_24_), channel_id=1, source_target_pairs={{0,16},{8,24},{16,0},{24,8},{1,17},{9,25},{17,1},{25,9},{2,18},{10... | collective-permute-start | bytes 2359304 | tf_op jit(solution)/shard_map/ppermute | solution.py:323
  166.2 32.4 %collective-permute-start.63 = (bf16[1024,384]{1,0:T(8,128)(2,1)S(1)}, bf16[1024,384]{1,0:T(8,128)(2,1)S(1)}, u32[]{:S(2)}, u32[]{:S(2)}) collective-permute-start(bf16[1024,384]{1,0:T(8,128)(2,1)S(1)} %constant_dynamic-update-slice_fusion.7.refs_24_), channel_id=1, source_target_pairs={{0,8},{8,0},{16,24},{24,16},{1,9},{9,1},{17,25},{25,17},{2,10},{10... | collective-permute-start | bytes 2359304 | tf_op jit(solution)/shard_map/ppermute | solution.py:323
  200.3 36.5 %collective-permute-start.27 = (bf16[1536,256]{1,0:T(8,128)(2,1)S(1)}, bf16[1536,256]{1,0:T(8,128)(2,1)}, u32[]{:S(2)}, u32[]{:S(2)}) collective-permute-start(bf16[1536,256]{1,0:T(8,128)(2,1)S(1)} %copy-done.10), channel_id=1, source_target_pairs={{0,4},{2,6},{4,0},{6,2},{1,5},{3,7},{5,1},{7,3},{8,12},{10,14},{12... | collective-permute-start | bytes 2359304 | tf_op jit(solution)/shard_map/ppermute | solution.py:307
  200.9 36.0 %collective-permute-start.28 = (bf16[1536,256]{1,0:T(8,128)(2,1)S(1)}, bf16[1536,256]{1,0:T(8,128)(2,1)}, u32[]{:S(2)}, u32[]{:S(2)}) collective-permute-start(bf16[1536,256]{1,0:T(8,128)(2,1)S(1)} %copy-done.10), channel_id=1, source_target_pairs={{0,6},{2,4},{4,2},{6,0},{1,7},{3,5},{5,3},{7,1},{8,14},{10,12},{12... | collective-permute-start | bytes 2359304 | tf_op jit(solution)/shard_map/ppermute | solution.py:307
  203.0 34.4 %collective-permute-start.29 = (bf16[1536,256]{1,0:T(8,128)(2,1)S(1)}, bf16[1536,256]{1,0:T(8,128)(2,1)S(1)}, u32[]{:S(2)}, u32[]{:S(2)}) collective-permute-start(bf16[1536,256]{1,0:T(8,128)(2,1)S(1)} %copy-done.10), channel_id=1, source_target_pairs={{1,0},{0,1},{3,2},{2,3},{5,4},{4,5},{7,6},{6,7},{9,8},{8,9},{11,10... | collective-permute-start | bytes 2359304 | tf_op jit(solution)/shard_map/ppermute | solution.py:319
  203.0 47.0 %collective-permute-start.66 = (bf16[1024,384]{1,0:T(8,128)(2,1)S(1)}, bf16[1024,384]{1,0:T(8,128)(2,1)S(1)}, u32[]{:S(2)}, u32[]{:S(2)}) collective-permute-start(bf16[1024,384]{1,0:T(8,128)(2,1)S(1)} %collective-permute-done.64.refs_26_), channel_id=1, source_target_pairs={{8,0},{16,24},{9,1},{17,25},{10,2},{18,26},{11,3},{19,27},{12,4},{... | collective-permute-start | bytes 2359304 | tf_op jit(solution)/shard_map/ppermute | solution.py:323
  215.2 36.5 %collective-permute-start.30 = (bf16[1536,256]{1,0:T(8,128)(2,1)S(1)}, bf16[1536,256]{1,0:T(8,128)(2,1)S(1)}, u32[]{:S(2)}, u32[]{:S(2)}) collective-permute-start(bf16[1536,256]{1,0:T(8,128)(2,1)S(1)} %collective-permute-done.26.refs_1_), channel_id=1, source_target_pairs={{1,0},{0,1},{3,2},{2,3},{5,4},{4,5},{7,6},{6,7},{9,8},{8,9},{11,10... | collective-permute-start | bytes 2359304 | tf_op jit(solution)/shard_map/ppermute | solution.py:319
  237.4 36.6 %collective-permute-start.53 = (bf16[1024,512]{1,0:T(8,128)(2,1)S(1)}, bf16[1024,512]{1,0:T(8,128)(2,1)S(1)}, u32[]{:S(2)}, u32[]{:S(2)}) collective-permute-start(bf16[1024,512]{1,0:T(8,128)(2,1)S(1)} %constant_dynamic-update-slice_fusion.3.refs_24_), channel_id=1, source_target_pairs={{0,8},{8,0},{16,24},{24,16},{1,9},{9,1},{17,25},{25,17},{2,10},{10... | collective-permute-start | bytes 3145736 | tf_op jit(solution)/shard_map/ppermute | solution.py:323
  252.6 43.3 %collective-permute-start.56 = (bf16[1024,512]{1,0:T(8,128)(2,1)}, bf16[1024,512]{1,0:T(8,128)(2,1)}, u32[]{:S(2)}, u32[]{:S(2)}) collective-permute-start(bf16[1024,512]{1,0:T(8,128)(2,1)} %collective-permute-done.54.refs_26_), channel_id=1, source_target_pairs={{8,0},{16,24},{9,1},{17,25},{10,2},{18,26},{11,3},{19,27},{12,4},{... | collective-permute-start | bytes 3145736 | tf_op jit(solution)/shard_map/ppermute | solution.py:323
  269.2 43.6 %collective-permute-start.67 = (bf16[384,384]{1,0:T(8,128)(2,1)}, bf16[384,384]{1,0:T(8,128)(2,1)S(1)}, u32[]{:S(2)}, u32[]{:S(2)}) collective-permute-start(bf16[384,384]{1,0:T(8,128)(2,1)} %get-tuple-element.70), channel_id=1, source_target_pairs={{0,2},{2,0},{4,6},{6,4},{1,3},{3,1},{5,7},{7,5},{8,10},{10,8},{12,... | collective-permute-start | bytes 884744 | tf_op jit(solution)/shard_map/ppermute | solution.py:307
  270.2 44.2 %collective-permute-start.68 = (bf16[384,384]{1,0:T(8,128)(2,1)}, bf16[384,384]{1,0:T(8,128)(2,1)S(1)}, u32[]{:S(2)}, u32[]{:S(2)}) collective-permute-start(bf16[384,384]{1,0:T(8,128)(2,1)} %get-tuple-element.71), channel_id=1, source_target_pairs={{0,4},{2,6},{4,0},{6,2},{1,5},{3,7},{5,1},{7,3},{8,12},{10,14},{12... | collective-permute-start | bytes 884744 | tf_op jit(solution)/shard_map/ppermute | solution.py:307
  275.0 39.5 %collective-permute-start.69 = (bf16[384,384]{1,0:T(8,128)(2,1)}, bf16[384,384]{1,0:T(8,128)(2,1)S(1)}, u32[]{:S(2)}, u32[]{:S(2)}) collective-permute-start(bf16[384,384]{1,0:T(8,128)(2,1)} %get-tuple-element.72), channel_id=1, source_target_pairs={{0,6},{2,4},{4,2},{6,0},{1,7},{3,5},{5,3},{7,1},{8,14},{10,12},{12... | collective-permute-start | bytes 884744 | tf_op jit(solution)/shard_map/ppermute | solution.py:307
  (103 other events, 2494.0 us)

commit v3 on v2

--- a/solution.py
+++ b/solution.py
@@ -62,10 +62,10 @@
     )(place, *arrays)
 
 
-def attention_kernel(place, *refs, planes, group, cols, rate, parts):
+def attention_kernel(place, *refs, planes, group, cols, layout, rate, parts):
     q_refs, refs = refs[:group], refs[group:]
     own, refs = refs[: cols * group], refs[cols * group :]
-    before, refs = refs[: cols * group], refs[cols * group :]
+    before, refs = refs[: cols * len(layout)], refs[cols * len(layout) :]
     w_refs, refs = refs[:planes], refs[planes:]
     o_ref, q_sc, w_sc, kv_sc, m_sc, acc_sc, before_sc, sems = refs
     grp, mem, col = place[0], place[1], place[2]
@@ -78,9 +78,12 @@
     depth = w_refs[0].shape[1]
 
     first_step = jnp.logical_and(pl.program_id(0) == 0, block == 0)
-    copies = [
-        pltpu.make_async_copy(before[i], before_sc.at[i], sems.at[i]) for i in range(cols * group)
-    ]
+    copies = []
+    for s in range(cols):
+        for i, (m, start, count) in enumerate(layout):
+            at = s * len(layout) + i
+            target = before_sc.at[s * group + m, pl.ds(start, count), :]
+            copies.append(pltpu.make_async_copy(before[at], target, sems.at[at]))
 
     @pl.when(first_step)
     def _():
@@ -171,7 +174,7 @@
     o_ref[...] = (acc_sc[:, :HEAD] / acc_sc[:, HEAD:]).astype(o_ref.dtype)
 
 
-def attention(place, queries, own, before, w, first_query, first_head, heads):
+def attention(place, queries, own, before, layout, w, first_query, first_head, heads):
     planes, group, cols = len(w), len(queries), len(own)
     tok, features = own[0][0].shape
     plane = tok * group
@@ -186,6 +189,7 @@
             planes=planes,
             group=group,
             cols=cols,
+            layout=layout,
             rate=HEAD**-0.5 * math.log2(math.e),
             parts=2,
         ),
@@ -206,7 +210,7 @@
                 pltpu.VMEM((size, HEAD), jnp.float32),
                 pltpu.VMEM((size, 2 * HEAD), jnp.float32),
                 pltpu.VMEM((cols * group, *before[0][0].shape), jnp.bfloat16),
-                pltpu.SemaphoreType.DMA((cols * group,)),
+                pltpu.SemaphoreType.DMA((cols * len(layout),)),
             ],
         ),
         compiler_params=pltpu.CompilerParams(
@@ -359,7 +363,17 @@
         return [x] + [plane_swap(x, k) for k in middle_shifts] + [plane_swap(x, far_shift, near)]
 
     out_first = spread(w_first)
-    below = gather(jnp.concatenate(lower))
+    below = jnp.concatenate(lower)
+    count = below.shape[0]
+    if group == 4:
+        cut_at = count // 32 * 16
+        ones, twos = swap(below, 1), swap(below, 2)
+        below = [below, ones, twos]
+        below += [swap(ones[:cut_at], 2), swap(twos[cut_at:], 1)]
+        layout = [(0, 0, count), (1, 0, count), (2, 0, count), (3, 0, cut_at), (3, cut_at, count - cut_at)]
+    else:
+        below = gather(below)
+        layout = [(m, 0, count) for m in shifts]
     my_queries = [exchange(blocks[(3 + t) * group : (4 + t) * group]) for t in range(turns)]
     w_second = exchange(blocks[2 * group : 3 * group])
 
@@ -372,7 +386,7 @@
     done = []
     for turn, first_head, heads in calls:
         i = len(done)
-        done.append(attention(place, my_queries[turn], owns, belows, w_all, first_head - turn * run, first_head, heads))
+        done.append(attention(place, my_queries[turn], owns, belows, layout, w_all, first_head - turn * run, first_head, heads))
         results[turn].append(gather(done[-1]))
         if i == 0:
             w_second, _ = lax.optimization_barrier((w_second, done[0]))

time: 334 us -> 342 us (1.024)
  starting transfers between devices: 109 us -> 117 us
    ppermute x36 -> x37, waiting for transfers between devices: 73.4 us -> 84.2 us  [swap(): return lax.ppermute(x, 'mem', [(p, p ^ m) for p in range(group)])]
    ppermute x11, waiting for transfers between devices: 76.7 us -> 70.1 us  [plane_swap(): return lax.ppermute(x, 'grp', [(z, z ^ k) for z in senders])]
    ppermute x36 -> x37, starting transfers between devices: 41.1 us -> 46.6 us  [swap(): return lax.ppermute(x, 'mem', [(p, p ^ m) for p in range(group)])]
    ppermute x20 -> x21, waiting for transfers between devices: 6.05 us -> 2.36 us  [across(): return lax.ppermute(x, 'col', [((c + s) % cols, c) for c in range(cols)])]
  transfers between devices with their start and end apart: 70 -> 72, of which waited for: 25 -> 21; matrix products, arithmetic and copies ran while one was open for 1% -> 1% of each run, Pallas kernels for 18% -> 17%
where the time goes in v3:
time: 342 us
  waiting for transfers between devices  157 us (46%)
  starting transfers between devices  117 us (34%)
  Pallas kernels  59.1 us (17%)
  local copies, waits for them, and re-layouts  6.16 us (2%)
    ppermute x37, waiting for transfers between devices, swap(): return lax.ppermute(x, 'mem', [(p, p ^ m) for p in range(group)])  84.2 us
    ppermute x11, waiting for transfers between devices, plane_swap(): return lax.ppermute(x, 'grp', [(z, z ^ k) for z in senders])  70.1 us
    ppermute x11, starting transfers between devices, plane_swap(): return lax.ppermute(x, 'grp', [(z, z ^ k) for z in senders])  56.3 us
    ppermute x37, starting transfers between devices, swap(): return lax.ppermute(x, 'mem', [(p, p ^ m) for p in range(group)])  46.6 us
    pallas_call x2, Pallas kernels, project(): pl.pallas_call(functools.partial(project_kernel, counts=[len(some) for so...  29.5 us
    pallas_call x3, Pallas kernels, attention(): pl.pallas_call(functools.partial(attention_kernel, planes=planes, group=g...  24.6 us
    ppermute x3, starting transfers between devices, up(): return lax.ppermute(x, 'grp', [(z, z + k) for z in range(planes - k)])  10.8 us
  transfers between devices with their start and end apart: 72, of which 21 were waited for; matrix products, arithmetic and copies ran while one was open for 1% of the time, Pallas kernels for 17%

profile of v3, /device:TPU:0, one launch (start us, length us, event | category | flops | bytes accessed | tf_op | source)
XLA Modules:
  0.0 342.0 jit_solution(4727612405828585006)
XLA Ops:
  0.0 7.0 %collective-permute-start.10 = (bf16[384,256]{1,0:T(8,128)(2,1)}, bf16[384,256]{1,0:T(8,128)(2,1)S(1)}, u32[]{:S(2)}, u32[]{:S(2)}) collective-permute-start(bf16[384,256]{1,0:T(8,128)(2,1)} %refs_4_.5), channel_id=1, source_target_pairs={{0,24},{1,25},{2,26},{3,27},{4,28},{5,29},{6,30},{7,31}} | collective-permute-start | bytes 589832 | tf_op jit(solution)/shard_map/ppermute | solution.py:320
  11.4 5.0 %cut.1 = (bf16[32,1024]{1,0:T(8,128)(2,1)}, bf16[32,1024]{1,0:T(8,128)(2,1)}, bf16[32,1024]{1,0:T(8,128)(2,1)}, bf16[32,1024]{1,0:T(8,128)(2,1)}, bf16[256,512]{...) custom-call(s32[3]{0:T(128)} %pad_add_fusion.place, ...), custom_call_target="tpu_custom_call" | custom-call | bytes 7340032 | tf_op jit(solution)/shard_map/cut/pallas_call | solution.py:42
  30.9 3.1 collective-permute-done.4.refs_6_
  39.3 17.1 %collective-permute-done.36.refs_2_ = bf16[384,256]{1,0:T(8,128)(2,1)S(1)} collective-permute-done((bf16[384,256]{1,0:T(8,128)(2,1)}, bf16[384,256]{1,0:T(8,128)(2,1)S(1)}, u32[]{:S(2)}, u32[]{:S(2)}) %collective-permute-start.36) | collective-permute-done | bytes 196640 | tf_op jit(solution)/shard_map/ppermute | solution.py:311
  56.4 3.2 collective-permute-start.54
  60.6 6.7 %collective-permute-done.53 = bf16[256,512]{1,0:T(8,128)(2,1)S(1)} collective-permute-done((bf16[256,512]{1,0:T(8,128)(2,1)}, bf16[256,512]{1,0:T(8,128)(2,1)S(1)}, u32[]{:S(2)}, u32[]{:S(2)}) %collective-permute-start.53) | collective-permute-done | bytes 262176 | tf_op jit(solution)/shard_map/ppermute | solution.py:311
  71.7 8.9 %collective-permute-done.26.refs_24_ = bf16[4,32,1024]{2,1,0:T(8,128)(2,1)S(1)} collective-permute-done((bf16[4,32,1024]{2,1,0:T(8,128)(2,1)S(1)}, bf16[4,32,1024]{2,1,0:T(8,128)(2,1)S(1)}, u32[]{:S(2)}, u32[]{:S(2)}) %collective-permute-start.26) | collective-permute-done | bytes 262176 | tf_op jit(solution)/shard_map/ppermute | solution.py:327
  83.7 3.7 %collective-permute-done.15.refs_15_ = bf16[576,256]{1,0:T(8,128)(2,1)S(1)} collective-permute-done((bf16[576,256]{1,0:T(8,128)(2,1)S(1)}, bf16[576,256]{1,0:T(8,128)(2,1)S(1)}, u32[]{:S(2)}, u32[]{:S(2)}) %collective-permute-start.15) | collective-permute-done | bytes 294944 | tf_op jit(solution)/shard_map/ppermute | solution.py:311
  94.9 7.0 %attention.5.refs_9_ = bf16[1536,128]{1,0:T(8,128)(2,1)} custom-call(s32[3]{0:T(128)} %pad_add_fusion.place, bf16[384,256]{1,0:T(8,128)(2,1)} %get-tuple-element.47.refs_0_, bf16[384,256]{1,0:T(8,128)(2,1)} %copy-done.53, bf16[384,256]{1,0:T(8,128)(2,1)} %copy-done.54, bf16[384,256]{1,0:T(8,128)(2,1)} %copy-done.55, bf16[384,256]{1,0:T(8,128)(2,1)} %refs_4_.5, ...), custom_call_target="tpu_custom_call" | custom-call | flops 7247757312 | bytes 6291456 | tf_op jit(solution)/shard_map/attention/pallas_call | solution.py:186
  102.9 9.1 %collective-permute-start.56 = (bf16[1024,512]{1,0:T(8,128)(2,1)S(1)}, bf16[1024,512]{1,0:T(8,128)(2,1)}, u32[]{:S(2)}, u32[]{:S(2)}) collective-permute-start(bf16[1024,512]{1,0:T(8,128)(2,1)S(1)} %constant_dynamic-update-slice_fusion.3.refs_24_), channel_id=1, source_target_pairs={{0,16},{8,24},{16,0},{24,8},{1,17},{9,25},{17,1},{25,9},{2,18},{10... | collective-permute-start | bytes 3145736 | tf_op jit(solution)/shard_map/ppermute | solution.py:327
  113.3 10.5 %attention.3.refs_0_ = bf16[1536,256]{1,0:T(8,128)(2,1)} custom-call(s32[3]{0:T(128)} %pad_add_fusion.place, bf16[384,256]{1,0:T(8,128)(2,1)} %get-tuple-element.39.refs_0_, bf16[384,256]{1,0:T(8,128)(2,1)} %copy-done.58, bf16[384,256]{1,0:T(8,128)(2,1)} %copy-done.59, bf16[384,256]{1,0:T(8,128)(2,1)} %collective-permute-done.2.refs_3_, ...), custom_call_target="tpu_custom_call" | custom-call | flops 14495514624 | bytes 6291456 | tf_op jit(solution)/shard_map/attention/pallas_call | solution.py:186
  123.9 7.1 %attention.4.refs_8_ = bf16[1536,128]{1,0:T(8,128)(2,1)} custom-call(s32[3]{0:T(128)} %pad_add_fusion.place, bf16[384,256]{1,0:T(8,128)(2,1)} %get-tuple-element.47.refs_0_, bf16[384,256]{1,0:T(8,128)(2,1)} %copy-done.53, bf16[384,256]{1,0:T(8,128)(2,1)} %copy-done.54, bf16[384,256]{1,0:T(8,128)(2,1)} %copy-done.55, bf16[384,256]{1,0:T(8,128)(2,1)} %refs_4_.5, ...), custom_call_target="tpu_custom_call" | custom-call | flops 7247757312 | bytes 6291456 | tf_op jit(solution)/shard_map/attention/pallas_call | solution.py:186
  134.7 22.1 %collective-permute-done.56.refs_26_ = bf16[1024,512]{1,0:T(8,128)(2,1)} collective-permute-done((bf16[1024,512]{1,0:T(8,128)(2,1)S(1)}, bf16[1024,512]{1,0:T(8,128)(2,1)}, u32[]{:S(2)}, u32[]{:S(2)}) %collective-permute-start.56) | collective-permute-done | bytes 1048608 | tf_op jit(solution)/shard_map/ppermute | solution.py:327
  159.9 14.5 %collective-permute-start.66 = (bf16[1024,384]{1,0:T(8,128)(2,1)S(1)}, bf16[1024,384]{1,0:T(8,128)(2,1)S(1)}, u32[]{:S(2)}, u32[]{:S(2)}) collective-permute-start(bf16[1024,384]{1,0:T(8,128)(2,1)S(1)} %constant_dynamic-update-slice_fusion.7.refs_24_), channel_id=1, source_target_pairs={{0,16},{8,24},{16,0},{24,8},{1,17},{9,25},{17,1},{25,9},{2,18},{10... | collective-permute-start | bytes 2359304 | tf_op jit(solution)/shard_map/ppermute | solution.py:327
  174.4 13.1 %collective-permute-start.65 = (bf16[1024,384]{1,0:T(8,128)(2,1)S(1)}, bf16[1024,384]{1,0:T(8,128)(2,1)S(1)}, u32[]{:S(2)}, u32[]{:S(2)}) collective-permute-start(bf16[1024,384]{1,0:T(8,128)(2,1)S(1)} %constant_dynamic-update-slice_fusion.7.refs_24_), channel_id=1, source_target_pairs={{0,8},{8,0},{16,24},{24,16},{1,9},{9,1},{17,25},{25,17},{2,10},{10... | collective-permute-start | bytes 2359304 | tf_op jit(solution)/shard_map/ppermute | solution.py:327
  191.3 15.5 %collective-permute-done.66.refs_26_ = bf16[1024,384]{1,0:T(8,128)(2,1)S(1)} collective-permute-done((bf16[1024,384]{1,0:T(8,128)(2,1)S(1)}, bf16[1024,384]{1,0:T(8,128)(2,1)S(1)}, u32[]{:S(2)}, u32[]{:S(2)}) %collective-permute-start.66) | collective-permute-done | bytes 786464 | tf_op jit(solution)/shard_map/ppermute | solution.py:327
  213.4 10.8 %collective-permute-done.28.refs_1_ = bf16[1536,256]{1,0:T(8,128)(2,1)S(1)} collective-permute-done((bf16[1536,256]{1,0:T(8,128)(2,1)S(1)}, bf16[1536,256]{1,0:T(8,128)(2,1)S(1)}, u32[]{:S(2)}, u32[]{:S(2)}) %collective-permute-start.28) | collective-permute-done | bytes 786464 | tf_op jit(solution)/shard_map/ppermute | solution.py:311
  224.3 21.6 %collective-permute-done.29.refs_2_ = bf16[1536,256]{1,0:T(8,128)(2,1)} collective-permute-done((bf16[1536,256]{1,0:T(8,128)(2,1)S(1)}, bf16[1536,256]{1,0:T(8,128)(2,1)}, u32[]{:S(2)}, u32[]{:S(2)}) %collective-permute-start.29) | collective-permute-done | bytes 786464 | tf_op jit(solution)/shard_map/ppermute | solution.py:311
  246.4 12.1 %collective-permute-start.55 = (bf16[1024,512]{1,0:T(8,128)(2,1)S(1)}, bf16[1024,512]{1,0:T(8,128)(2,1)S(1)}, u32[]{:S(2)}, u32[]{:S(2)}) collective-permute-start(bf16[1024,512]{1,0:T(8,128)(2,1)S(1)} %constant_dynamic-update-slice_fusion.3.refs_24_), channel_id=1, source_target_pairs={{0,8},{8,0},{16,24},{24,16},{1,9},{9,1},{17,25},{25,17},{2,10},{10... | collective-permute-start | bytes 3145736 | tf_op jit(solution)/shard_map/ppermute | solution.py:327
  263.2 14.6 %project.3 = (bf16[384,384]{1,0:T(8,128)(2,1)}, bf16[384,384]{1,0:T(8,128)(2,1)}, bf16[384,384]{1,0:T(8,128)(2,1)}, bf16[384,384]{1,0:T(8,128)(2,1)}) custom-call(s32[6]{0:T(128)} %stack.86.scalars, bf16[1536,256]{1,0:T(8,128)(2,1)} %attention.3.refs_0_, bf16[1536,256]{1,0:T(8,128)(2,1)} %copy-done.14, bf16[1536,256]{1,0:T(8,128)(2,1)} %collective-permute-done.29.refs_2_, ...), custom_call_target="tpu_custom_call" | custom-call | flops 4831838208 | bytes 15728640 | tf_op jit(solution)/shard_map/project/pallas_call | solution.py:271
  284.9 19.6 %collective-permute-done.58.refs_28_ = bf16[1024,512]{1,0:T(8,128)(2,1)} collective-permute-done((bf16[1024,512]{1,0:T(8,128)(2,1)}, bf16[1024,512]{1,0:T(8,128)(2,1)}, u32[]{:S(2)}, u32[]{:S(2)}) %collective-permute-start.58) | collective-permute-done | bytes 1048608 | tf_op jit(solution)/shard_map/ppermute | solution.py:327
  304.5 14.9 %project.2 = (bf16[384,512]{1,0:T(8,128)(2,1)}, bf16[384,512]{1,0:T(8,128)(2,1)}, bf16[384,512]{1,0:T(8,128)(2,1)}, bf16[384,512]{1,0:T(8,128)(2,1)}) custom-call(s32[6]{0:T(128)} %stack.86.scalars, bf16[1536,256]{1,0:T(8,128)(2,1)} %attention.3.refs_0_, bf16[1536,256]{1,0:T(8,128)(2,1)} %copy-done.14, bf16[1536,256]{1,0:T(8,128)(2,1)} %collective-permute-done.29.refs_2_, ...), custom_call_target="tpu_custom_call" | custom-call | flops 6442450944 | bytes 16777216 | tf_op jit(solution)/shard_map/project/pallas_call | solution.py:271
  323.2 8.5 %collective-permute-done.59 = bf16[384,512]{1,0:T(8,128)(2,1)S(1)} collective-permute-done((bf16[384,512]{1,0:T(8,128)(2,1)}, bf16[384,512]{1,0:T(8,128)(2,1)S(1)}, u32[]{:S(2)}, u32[]{:S(2)}) %collective-permute-start.59) | collective-permute-done | bytes 393248 | tf_op jit(solution)/shard_map/ppermute | solution.py:311
  331.7 7.5 %collective-permute-done.60 = bf16[384,512]{1,0:T(8,128)(2,1)S(1)} collective-permute-done((bf16[384,512]{1,0:T(8,128)(2,1)}, bf16[384,512]{1,0:T(8,128)(2,1)S(1)}, u32[]{:S(2)}, u32[]{:S(2)}) %collective-permute-start.60) | collective-permute-done | bytes 393248 | tf_op jit(solution)/shard_map/ppermute | solution.py:311
  (272 shorter events, 78.0 us)
Async XLA Ops:
  29.4 41.6 %collective-permute-start.13 = (bf16[1152,256]{1,0:T(8,128)(2,1)S(1)}, bf16[1152,256]{1,0:T(8,128)(2,1)S(1)}, u32[]{:S(2)}, u32[]{:S(2)}) collective-permute-start(bf16[1152,256]{1,0:T(8,128)(2,1)S(1)} %constant_dynamic-update-slice_fusion.refs_12_), channel_id=1, source_target_pairs={{0,2},{2,0},{4,6},{6,4},{1,3},{3,1},{5,7},{7,5},{8,10},{10,8},{12,... | collective-permute-start | bytes 1769480 | tf_op jit(solution)/shard_map/ppermute | solution.py:311
  34.0 37.6 %collective-permute-start.14 = (bf16[1152,256]{1,0:T(8,128)(2,1)S(1)}, bf16[1152,256]{1,0:T(8,128)(2,1)S(1)}, u32[]{:S(2)}, u32[]{:S(2)}) collective-permute-start(bf16[1152,256]{1,0:T(8,128)(2,1)S(1)} %constant_dynamic-update-slice_fusion.refs_12_), channel_id=1, source_target_pairs={{0,4},{2,6},{4,0},{6,2},{1,5},{3,7},{5,1},{7,3},{8,12},{10,14},{12... | collective-permute-start | bytes 1769480 | tf_op jit(solution)/shard_map/ppermute | solution.py:311
  92.1 38.9 %collective-permute-start.62 = (bf16[256,384]{1,0:T(8,128)(2,1)}, bf16[256,384]{1,0:T(8,128)(2,1)S(1)}, u32[]{:S(2)}, u32[]{:S(2)}) collective-permute-start(bf16[256,384]{1,0:T(8,128)(2,1)} %get-tuple-element.61), channel_id=1, source_target_pairs={{0,2},{2,0},{4,6},{6,4},{1,3},{3,1},{5,7},{7,5},{8,10},{10,8},{12,... | collective-permute-start | bytes 589832 | tf_op jit(solution)/shard_map/ppermute | solution.py:311
  93.7 38.7 %collective-permute-start.63 = (bf16[256,384]{1,0:T(8,128)(2,1)}, bf16[256,384]{1,0:T(8,128)(2,1)S(1)}, u32[]{:S(2)}, u32[]{:S(2)}) collective-permute-start(bf16[256,384]{1,0:T(8,128)(2,1)} %get-tuple-element.62), channel_id=1, source_target_pairs={{0,4},{2,6},{4,0},{6,2},{1,5},{3,7},{5,1},{7,3},{8,12},{10,14},{12... | collective-permute-start | bytes 589832 | tf_op jit(solution)/shard_map/ppermute | solution.py:311
  102.0 31.2 %collective-permute-start.64 = (bf16[256,384]{1,0:T(8,128)(2,1)S(1)}, bf16[256,384]{1,0:T(8,128)(2,1)S(1)}, u32[]{:S(2)}, u32[]{:S(2)}) collective-permute-start(bf16[256,384]{1,0:T(8,128)(2,1)S(1)} %copy-done.45), channel_id=1, source_target_pairs={{0,6},{2,4},{4,2},{6,0},{1,7},{3,5},{5,3},{7,1},{8,14},{10,12},{12... | collective-permute-start | bytes 589832 | tf_op jit(solution)/shard_map/ppermute | solution.py:311
  102.9 53.9 %collective-permute-start.56 = (bf16[1024,512]{1,0:T(8,128)(2,1)S(1)}, bf16[1024,512]{1,0:T(8,128)(2,1)}, u32[]{:S(2)}, u32[]{:S(2)}) collective-permute-start(bf16[1024,512]{1,0:T(8,128)(2,1)S(1)} %constant_dynamic-update-slice_fusion.3.refs_24_), channel_id=1, source_target_pairs={{0,16},{8,24},{16,0},{24,8},{1,17},{9,25},{17,1},{25,9},{2,18},{10... | collective-permute-start | bytes 3145736 | tf_op jit(solution)/shard_map/ppermute | solution.py:327
  112.0 45.9 %collective-permute-start.39 = (bf16[1536,128]{1,0:T(8,128)(2,1)}, bf16[1536,128]{1,0:T(8,128)(2,1)S(1)}, u32[]{:S(2)}, u32[]{:S(2)}) collective-permute-start(bf16[1536,128]{1,0:T(8,128)(2,1)} %attention.5.refs_9_), channel_id=1, source_target_pairs={{0,2},{2,0},{4,6},{6,4},{1,3},{3,1},{5,7},{7,5},{8,10},{10,8},{12,... | collective-permute-start | bytes 1179656 | tf_op jit(solution)/shard_map/ppermute | solution.py:311
  131.0 28.8 %collective-permute-start.41 = (bf16[1536,128]{1,0:T(8,128)(2,1)S(1)}, bf16[1536,128]{1,0:T(8,128)(2,1)S(1)}, u32[]{:S(2)}, u32[]{:S(2)}) collective-permute-start(bf16[1536,128]{1,0:T(8,128)(2,1)S(1)} %copy-done.23), channel_id=1, source_target_pairs={{0,4},{2,6},{4,0},{6,2},{1,5},{3,7},{5,1},{7,3},{8,12},{10,14},{12... | collective-permute-start | bytes 1179656 | tf_op jit(solution)/shard_map/ppermute | solution.py:311
  132.4 42.0 %collective-permute-start.43 = (bf16[1536,128]{1,0:T(8,128)(2,1)S(1)}, bf16[1536,128]{1,0:T(8,128)(2,1)S(1)}, u32[]{:S(2)}, u32[]{:S(2)}) collective-permute-start(bf16[1536,128]{1,0:T(8,128)(2,1)S(1)} %copy-done.23), channel_id=1, source_target_pairs={{0,6},{2,4},{4,2},{6,0},{1,7},{3,5},{5,3},{7,1},{8,14},{10,12},{12... | collective-permute-start | bytes 1179656 | tf_op jit(solution)/shard_map/ppermute | solution.py:311
  133.3 54.2 %collective-permute-start.38 = (bf16[1536,128]{1,0:T(8,128)(2,1)}, bf16[1536,128]{1,0:T(8,128)(2,1)S(1)}, u32[]{:S(2)}, u32[]{:S(2)}) collective-permute-start(bf16[1536,128]{1,0:T(8,128)(2,1)} %attention.4.refs_8_), channel_id=1, source_target_pairs={{0,2},{2,0},{4,6},{6,4},{1,3},{3,1},{5,7},{7,5},{8,10},{10,8},{12,... | collective-permute-start | bytes 1179656 | tf_op jit(solution)/shard_map/ppermute | solution.py:311
  156.8 31.3 %collective-permute-start.40 = (bf16[1536,128]{1,0:T(8,128)(2,1)}, bf16[1536,128]{1,0:T(8,128)(2,1)S(1)}, u32[]{:S(2)}, u32[]{:S(2)}) collective-permute-start(bf16[1536,128]{1,0:T(8,128)(2,1)} %attention.4.refs_8_), channel_id=1, source_target_pairs={{0,4},{2,6},{4,0},{6,2},{1,5},{3,7},{5,1},{7,3},{8,12},{10,14},{12... | collective-permute-start | bytes 1179656 | tf_op jit(solution)/shard_map/ppermute | solution.py:311
  157.9 30.4 %collective-permute-start.42 = (bf16[1536,128]{1,0:T(8,128)(2,1)}, bf16[1536,128]{1,0:T(8,128)(2,1)S(1)}, u32[]{:S(2)}, u32[]{:S(2)}) collective-permute-start(bf16[1536,128]{1,0:T(8,128)(2,1)} %attention.4.refs_8_), channel_id=1, source_target_pairs={{0,6},{2,4},{4,2},{6,0},{1,7},{3,5},{5,3},{7,1},{8,14},{10,12},{12... | collective-permute-start | bytes 1179656 | tf_op jit(solution)/shard_map/ppermute | solution.py:311
  159.9 46.9 %collective-permute-start.66 = (bf16[1024,384]{1,0:T(8,128)(2,1)S(1)}, bf16[1024,384]{1,0:T(8,128)(2,1)S(1)}, u32[]{:S(2)}, u32[]{:S(2)}) collective-permute-start(bf16[1024,384]{1,0:T(8,128)(2,1)S(1)} %constant_dynamic-update-slice_fusion.7.refs_24_), channel_id=1, source_target_pairs={{0,16},{8,24},{16,0},{24,8},{1,17},{9,25},{17,1},{25,9},{2,18},{10... | collective-permute-start | bytes 2359304 | tf_op jit(solution)/shard_map/ppermute | solution.py:327
  174.4 33.3 %collective-permute-start.65 = (bf16[1024,384]{1,0:T(8,128)(2,1)S(1)}, bf16[1024,384]{1,0:T(8,128)(2,1)S(1)}, u32[]{:S(2)}, u32[]{:S(2)}) collective-permute-start(bf16[1024,384]{1,0:T(8,128)(2,1)S(1)} %constant_dynamic-update-slice_fusion.7.refs_24_), channel_id=1, source_target_pairs={{0,8},{8,0},{16,24},{24,16},{1,9},{9,1},{17,25},{25,17},{2,10},{10... | collective-permute-start | bytes 2359304 | tf_op jit(solution)/shard_map/ppermute | solution.py:327
  209.4 36.5 %collective-permute-start.29 = (bf16[1536,256]{1,0:T(8,128)(2,1)S(1)}, bf16[1536,256]{1,0:T(8,128)(2,1)}, u32[]{:S(2)}, u32[]{:S(2)}) collective-permute-start(bf16[1536,256]{1,0:T(8,128)(2,1)S(1)} %copy-done.12), channel_id=1, source_target_pairs={{0,4},{2,6},{4,0},{6,2},{1,5},{3,7},{5,1},{7,3},{8,12},{10,14},{12... | collective-permute-start | bytes 2359304 | tf_op jit(solution)/shard_map/ppermute | solution.py:311
  210.5 35.4 %collective-permute-start.30 = (bf16[1536,256]{1,0:T(8,128)(2,1)S(1)}, bf16[1536,256]{1,0:T(8,128)(2,1)}, u32[]{:S(2)}, u32[]{:S(2)}) collective-permute-start(bf16[1536,256]{1,0:T(8,128)(2,1)S(1)} %copy-done.12), channel_id=1, source_target_pairs={{0,6},{2,4},{4,2},{6,0},{1,7},{3,5},{5,3},{7,1},{8,14},{10,12},{12... | collective-permute-start | bytes 2359304 | tf_op jit(solution)/shard_map/ppermute | solution.py:311
  212.0 34.4 %collective-permute-start.31 = (bf16[1536,256]{1,0:T(8,128)(2,1)S(1)}, bf16[1536,256]{1,0:T(8,128)(2,1)S(1)}, u32[]{:S(2)}, u32[]{:S(2)}) collective-permute-start(bf16[1536,256]{1,0:T(8,128)(2,1)S(1)} %copy-done.12), channel_id=1, source_target_pairs={{1,0},{0,1},{3,2},{2,3},{5,4},{4,5},{7,6},{6,7},{9,8},{8,9},{11,10... | collective-permute-start | bytes 2359304 | tf_op jit(solution)/shard_map/ppermute | solution.py:323
  212.1 46.4 %collective-permute-start.68 = (bf16[1024,384]{1,0:T(8,128)(2,1)S(1)}, bf16[1024,384]{1,0:T(8,128)(2,1)S(1)}, u32[]{:S(2)}, u32[]{:S(2)}) collective-permute-start(bf16[1024,384]{1,0:T(8,128)(2,1)S(1)} %collective-permute-done.66.refs_26_), channel_id=1, source_target_pairs={{8,0},{16,24},{9,1},{17,25},{10,2},{18,26},{11,3},{19,27},{12,4},{... | collective-permute-start | bytes 2359304 | tf_op jit(solution)/shard_map/ppermute | solution.py:327
  224.3 35.9 %collective-permute-start.32 = (bf16[1536,256]{1,0:T(8,128)(2,1)S(1)}, bf16[1536,256]{1,0:T(8,128)(2,1)S(1)}, u32[]{:S(2)}, u32[]{:S(2)}) collective-permute-start(bf16[1536,256]{1,0:T(8,128)(2,1)S(1)} %collective-permute-done.28.refs_1_), channel_id=1, source_target_pairs={{1,0},{0,1},{3,2},{2,3},{5,4},{4,5},{7,6},{6,7},{9,8},{8,9},{11,10... | collective-permute-start | bytes 2359304 | tf_op jit(solution)/shard_map/ppermute | solution.py:323
  246.4 36.1 %collective-permute-start.55 = (bf16[1024,512]{1,0:T(8,128)(2,1)S(1)}, bf16[1024,512]{1,0:T(8,128)(2,1)S(1)}, u32[]{:S(2)}, u32[]{:S(2)}) collective-permute-start(bf16[1024,512]{1,0:T(8,128)(2,1)S(1)} %constant_dynamic-update-slice_fusion.3.refs_24_), channel_id=1, source_target_pairs={{0,8},{8,0},{16,24},{24,16},{1,9},{9,1},{17,25},{25,17},{2,10},{10... | collective-permute-start | bytes 3145736 | tf_op jit(solution)/shard_map/ppermute | solution.py:327
  261.2 43.3 %collective-permute-start.58 = (bf16[1024,512]{1,0:T(8,128)(2,1)}, bf16[1024,512]{1,0:T(8,128)(2,1)}, u32[]{:S(2)}, u32[]{:S(2)}) collective-permute-start(bf16[1024,512]{1,0:T(8,128)(2,1)} %collective-permute-done.56.refs_26_), channel_id=1, source_target_pairs={{8,0},{16,24},{9,1},{17,25},{10,2},{18,26},{11,3},{19,27},{12,4},{... | collective-permute-start | bytes 3145736 | tf_op jit(solution)/shard_map/ppermute | solution.py:327
  277.8 43.7 %collective-permute-start.69 = (bf16[384,384]{1,0:T(8,128)(2,1)}, bf16[384,384]{1,0:T(8,128)(2,1)S(1)}, u32[]{:S(2)}, u32[]{:S(2)}) collective-permute-start(bf16[384,384]{1,0:T(8,128)(2,1)} %get-tuple-element.70), channel_id=1, source_target_pairs={{0,2},{2,0},{4,6},{6,4},{1,3},{3,1},{5,7},{7,5},{8,10},{10,8},{12,... | collective-permute-start | bytes 884744 | tf_op jit(solution)/shard_map/ppermute | solution.py:311
  278.7 44.3 %collective-permute-start.70 = (bf16[384,384]{1,0:T(8,128)(2,1)}, bf16[384,384]{1,0:T(8,128)(2,1)S(1)}, u32[]{:S(2)}, u32[]{:S(2)}) collective-permute-start(bf16[384,384]{1,0:T(8,128)(2,1)} %get-tuple-element.71), channel_id=1, source_target_pairs={{0,4},{2,6},{4,0},{6,2},{1,5},{3,7},{5,1},{7,3},{8,12},{10,14},{12... | collective-permute-start | bytes 884744 | tf_op jit(solution)/shard_map/ppermute | solution.py:311
  283.5 39.5 %collective-permute-start.71 = (bf16[384,384]{1,0:T(8,128)(2,1)}, bf16[384,384]{1,0:T(8,128)(2,1)S(1)}, u32[]{:S(2)}, u32[]{:S(2)}) collective-permute-start(bf16[384,384]{1,0:T(8,128)(2,1)} %get-tuple-element.72), channel_id=1, source_target_pairs={{0,6},{2,4},{4,2},{6,0},{1,7},{3,5},{5,3},{7,1},{8,14},{10,12},{12... | collective-permute-start | bytes 884744 | tf_op jit(solution)/shard_map/ppermute | solution.py:311
  (108 other events, 2436.7 us)

commit v4 on v3

--- a/solution.py
+++ b/solution.py
@@ -225,77 +225,95 @@
     )(place, *queries, *(x for some in own for x in some), *(x for some in before for x in some), *w)
 
 
-def project_kernel(scalars, *refs, counts, group, planes):
+def project_kernel(scalars, *refs, counts, group, planes, carried, last):
     a_refs, refs = refs[: sum(counts)], refs[sum(counts) :]
     b_refs, refs = refs[: planes + 1], refs[planes + 1 :]
-    outs, (b_sc, sems) = refs[:group], refs[group:]
+    if carried:
+        part_ref, refs = refs[0], refs[1:]
+    outs, (b_sc, sems) = refs[:-2], refs[-2:]
     step = pl.program_id(0)
     near = scalars[len(counts) + 1] == 1
 
+    for x in range(len(counts)):
+        for k in range(planes + 1):
+            slot = min(k, planes - 1)
+            wanted = jnp.logical_and(step == 0, scalars[x] == slot)
+            if k >= planes - 1:
+                wanted = jnp.logical_and(wanted, near if k == planes - 1 else jnp.logical_not(near))
+
+            @pl.when(wanted)
+            def _():
+                pltpu.make_async_copy(b_refs[k], b_sc.at[x], sems.at[x]).start()
+
     @pl.when(step == 0)
     def _():
-        copies = [pltpu.make_async_copy(b_refs[k], b_sc.at[k], sems.at[k]) for k in range(planes - 1)]
-        for copy in copies:
-            copy.start()
-        for which, source in ((near, b_refs[planes - 1]), (jnp.logical_not(near), b_refs[planes])):
-
-            @pl.when(which)
-            def _():
-                copy = pltpu.make_async_copy(source, b_sc.at[planes - 1], sems.at[planes - 1])
-                copy.start()
-                copy.wait()
-
-        for copy in copies:
-            copy.wait()
-
-    out, at = None, 0
+        for x in range(len(counts)):
+            pltpu.make_async_copy(b_refs[0], b_sc.at[x], sems.at[x]).wait()
+
+    out, at = part_ref[...] if carried else None, 0
     for x, count in enumerate(counts):
         heads = [a_refs[at + i][...] for i in range(count)]
         a = heads[0] if count == 1 else jnp.concatenate(heads, axis=1)
-        term = jnp.dot(a, b_sc[scalars[x]], preferred_element_type=jnp.float32)
+        term = jnp.dot(a, b_sc[x], preferred_element_type=jnp.float32)
         out = term if out is None else out + term
         at += count
-    for m in range(group):
-
-        @pl.when(step == m)
-        def _():
-            outs[m][...] = out.astype(outs[m].dtype)
-
-
-def project(scalars, sets, blocks, group):
+    if last:
+        for m in range(group):
+
+            @pl.when(step == m)
+            def _():
+                outs[m][...] = out.astype(outs[m].dtype)
+    else:
+        outs[0][...] = out
+
+
+def project(meets, mem, is_near, sets, blocks, group, carried=None, last=True):
+    scalars = jnp.stack([*meets, mem, is_near]).astype(jnp.int32)
     pieces = [x for some in sets for x in some]
     planes = len(blocks) - 1
-    tok = pieces[0].shape[0] // group
+    rows = pieces[0].shape[0]
+    tok = rows // group
     depth, width = blocks[0].shape
     count = len(sets)
-    return pl.pallas_call(
+    part_spec = pl.BlockSpec((tok, width), lambda j, s: (j, 0))
+    parts = [] if carried is None else [carried]
+    out = pl.pallas_call(
         functools.partial(
-            project_kernel, counts=[len(some) for some in sets], group=group, planes=planes
-        ),
-        out_shape=[jax.ShapeDtypeStruct((tok, width), jnp.bfloat16)] * group,
+            project_kernel,
+            counts=[len(some) for some in sets],
+            group=group,
+            planes=planes,
+            carried=carried is not None,
+            last=last,
+        ),
+        out_shape=[jax.ShapeDtypeStruct((tok, width), jnp.bfloat16)] * group
+        if last
+        else [jax.ShapeDtypeStruct((rows, width), jnp.float32)],
         grid_spec=pltpu.PrefetchScalarGridSpec(
             num_scalar_prefetch=1,
             grid=(group,),
             in_specs=[
                 pl.BlockSpec((tok, x.shape[1]), lambda j, s: (s[count] ^ j, 0)) for x in pieces
             ]
-            + [pl.BlockSpec(memory_space=pl.ANY) for _ in blocks],
-            out_specs=[pl.BlockSpec((tok, width), lambda j, s: (0, 0))] * group,
+            + [pl.BlockSpec(memory_space=pl.ANY) for _ in blocks]
+            + [part_spec for _ in parts],
+            out_specs=[pl.BlockSpec((tok, width), lambda j, s: (0, 0))] * group if last else [part_spec],
             scratch_shapes=[
-                pltpu.VMEM((planes, depth, width), jnp.bfloat16),
-                pltpu.SemaphoreType.DMA((planes,)),
+                pltpu.VMEM((count, depth, width), jnp.bfloat16),
+                pltpu.SemaphoreType.DMA((count,)),
             ],
         ),
         compiler_params=pltpu.CompilerParams(
             dimension_semantics=("arbitrary",), vmem_limit_bytes=VMEM_LIMIT
         ),
         cost_estimate=pl.CostEstimate(
-            flops=2 * tok * group * planes * depth * width,
+            flops=2 * rows * count * depth * width,
             transcendentals=0,
-            bytes_accessed=planes * depth * width * 2 + tok * group * planes * depth * 2,
+            bytes_accessed=count * depth * width * 2 + rows * count * depth * 2,
         ),
         name="project",
-    )(scalars, *pieces, *blocks)
+    )(scalars, *pieces, *blocks, *parts)
+    return out if last else out[0]
 
 
 def per_device(latent, w_kv, queries, w_out):
@@ -402,7 +420,6 @@
             some = [[x if s == 0 else across(x, s) for x in part] for part in results[turn]]
             sets.append([part[m] for m in shifts for part in some])
             meets.append((((col + s) % cols) * turns + turn) ^ grp)
-    scalars = jnp.stack([*meets, mem, is_near]).astype(jnp.int32)
 
     def in_order(out, last):
         by_shift = {0: out[0], half: out[1], far_shift: out[-1]}
@@ -411,7 +428,11 @@
 
     mixed = []
     for out, last in ((out_first, first_far), (out_second, second_far)):
-        columns = project(scalars, sets, in_order(out, last), group)
+        rows, part, early = in_order(out, last), None, 0
+        if not mixed and turns > 1:
+            early = cols * (turns - 1)
+            part = project(meets[:early], mem, is_near, sets[:early], rows, group, None, False)
+        columns = project(meets[early:], mem, is_near, sets[early:], rows, group, part)
         got = exchange(columns)
         stack = jnp.stack(got)
         mixed.append([lax.dynamic_index_in_dim(stack, mem ^ p, 0, False) for p in shifts])

time: 342 us -> 342 us (level)
  starting transfers between devices: 117 us -> 83.5 us
  waiting for transfers between devices: 157 us -> 180 us
  Pallas kernels: 59.1 us -> 64.5 us
    ppermute x11, waiting for transfers between devices: 70.1 us -> 106 us  [plane_swap(): return lax.ppermute(x, 'grp', [(z, z ^ k) for z in senders])]
    ppermute x11, starting transfers between devices: 56.3 us -> 23.8 us  [plane_swap(): return lax.ppermute(x, 'grp', [(z, z ^ k) for z in senders])]
    ppermute x37, waiting for transfers between devices: 84.2 us -> 72.4 us  [swap(): return lax.ppermute(x, 'mem', [(p, p ^ m) for p in range(group)])]
    pallas_call x2 -> x3, Pallas kernels: 29.5 us -> 34.9 us  [project(): pl.pallas_call(functools.partial(project_kernel, counts=[len(some) for so...]
    unnamed x135 -> x131, local copies, waits for them, and re-layouts: 4.64 us -> 7.36 us
  transfers between devices with their start and end apart: 72 -> 72, of which waited for: 21 -> 26; matrix products, arithmetic and copies ran while one was open for 1% -> 1% of each run, Pallas kernels for 17% -> 19%
where the time goes in v4:
time: 342 us
  waiting for transfers between devices  180 us (53%)
  starting transfers between devices  83.5 us (24%)
  Pallas kernels  64.5 us (19%)
  local copies, waits for them, and re-layouts  8.83 us (3%)
  other arithmetic  4.16 us (1%)
    ppermute x11, waiting for transfers between devices, plane_swap(): return lax.ppermute(x, 'grp', [(z, z ^ k) for z in senders])  106 us
    ppermute x37, waiting for transfers between devices, swap(): return lax.ppermute(x, 'mem', [(p, p ^ m) for p in range(group)])  72.4 us
    ppermute x37, starting transfers between devices, swap(): return lax.ppermute(x, 'mem', [(p, p ^ m) for p in range(group)])  46.2 us
    pallas_call x3, Pallas kernels, project(): pl.pallas_call(functools.partial(project_kernel, counts=[len(some) for so...  34.9 us
    pallas_call x3, Pallas kernels, attention(): pl.pallas_call(functools.partial(attention_kernel, planes=planes, group=g...  24.5 us
    ppermute x11, starting transfers between devices, plane_swap(): return lax.ppermute(x, 'grp', [(z, z ^ k) for z in senders])  23.8 us
    ppermute x3, starting transfers between devices, up(): return lax.ppermute(x, 'grp', [(z, z + k) for z in range(planes - k)])  10.7 us
    unnamed x131, local copies, waits for them, and re-layouts  7.36 us
  transfers between devices with their start and end apart: 72, of which 26 were waited for; matrix products, arithmetic and copies ran while one was open for 1% of the time, Pallas kernels for 19%

profile of v4, /device:TPU:0, one launch (start us, length us, event | category | flops | bytes accessed | tf_op | source)
XLA Modules:
  0.0 341.7 jit_solution(8798639512086505470)
XLA Ops:
  0.0 7.0 %collective-permute-start.10 = (bf16[384,256]{1,0:T(8,128)(2,1)}, bf16[384,256]{1,0:T(8,128)(2,1)S(1)}, u32[]{:S(2)}, u32[]{:S(2)}) collective-permute-start(bf16[384,256]{1,0:T(8,128)(2,1)} %refs_4_.5), channel_id=1, source_target_pairs={{0,24},{1,25},{2,26},{3,27},{4,28},{5,29},{6,30},{7,31}} | collective-permute-start | bytes 589832 | tf_op jit(solution)/shard_map/ppermute | solution.py:338
  11.5 5.0 %cut.1 = (bf16[32,1024]{1,0:T(8,128)(2,1)}, bf16[32,1024]{1,0:T(8,128)(2,1)}, bf16[32,1024]{1,0:T(8,128)(2,1)}, bf16[32,1024]{1,0:T(8,128)(2,1)}, bf16[256,512]{...) custom-call(s32[3]{0:T(128)} %pad_add_fusion.place, ...), custom_call_target="tpu_custom_call" | custom-call | bytes 7340032 | tf_op jit(solution)/shard_map/cut/pallas_call | solution.py:42
  18.0 3.2 collective-permute-done.22
  45.3 14.3 %collective-permute-done.2.refs_3_ = bf16[384,256]{1,0:T(8,128)(2,1)S(1)} collective-permute-done((bf16[384,256]{1,0:T(8,128)(2,1)}, bf16[384,256]{1,0:T(8,128)(2,1)S(1)}, u32[]{:S(2)}, u32[]{:S(2)}) %collective-permute-start.2) | collective-permute-done | bytes 196640 | tf_op jit(solution)/shard_map/ppermute | solution.py:329
  73.6 6.6 %collective-permute-done.27.refs_25_ = bf16[4,32,1024]{2,1,0:T(8,128)(2,1)S(1)} collective-permute-done((bf16[4,32,1024]{2,1,0:T(8,128)(2,1)S(1)}, bf16[4,32,1024]{2,1,0:T(8,128)(2,1)S(1)}, u32[]{:S(2)}, u32[]{:S(2)}) %collective-permute-start.27) | collective-permute-done | bytes 262176 | tf_op jit(solution)/shard_map/ppermute | solution.py:345
  80.9 8.1 %collective-permute-done.26.refs_24_ = bf16[4,32,1024]{2,1,0:T(8,128)(2,1)S(1)} collective-permute-done((bf16[4,32,1024]{2,1,0:T(8,128)(2,1)S(1)}, bf16[4,32,1024]{2,1,0:T(8,128)(2,1)S(1)}, u32[]{:S(2)}, u32[]{:S(2)}) %collective-permute-start.26) | collective-permute-done | bytes 262176 | tf_op jit(solution)/shard_map/ppermute | solution.py:345
  92.4 3.4 collective-permute-done.16.refs_16_
  103.7 7.0 %attention.3.refs_0_.refs_8_ = bf16[1536,128]{1,0:T(8,128)(2,1)} custom-call(s32[3]{0:T(128)} %pad_add_fusion.place, bf16[384,256]{1,0:T(8,128)(2,1)} %get-tuple-element.39.refs_0_, bf16[384,256]{1,0:T(8,128)(2,1)} %copy-done.51, bf16[384,256]{1,0:T(8,128)(2,1)} %copy-done.52, bf16[384,256]{1,0:T(8,128)(2,1)} %copy-done.53, bf16[384,256]{1,0:T(8,128)(2,1)} %refs_4_.5, ...), custom_call_target="tpu_custom_call" | custom-call | flops 7247757312 | bytes 6291456 | tf_op jit(solution)/shard_map/attention/pallas_call | solution.py:186
  114.7 6.9 %attention.4.refs_1_.refs_9_ = bf16[1536,128]{1,0:T(8,128)(2,1)} custom-call(s32[3]{0:T(128)} %pad_add_fusion.place, bf16[384,256]{1,0:T(8,128)(2,1)} %get-tuple-element.39.refs_0_, bf16[384,256]{1,0:T(8,128)(2,1)} %copy-done.51, bf16[384,256]{1,0:T(8,128)(2,1)} %copy-done.52, bf16[384,256]{1,0:T(8,128)(2,1)} %copy-done.53, bf16[384,256]{1,0:T(8,128)(2,1)} %refs_4_.5, ...), custom_call_target="tpu_custom_call" | custom-call | flops 7247757312 | bytes 6291456 | tf_op jit(solution)/shard_map/attention/pallas_call | solution.py:186
  122.3 28.3 %collective-permute-done.46.refs_10_.refs_18_ = bf16[1024,512]{1,0:T(8,128)(2,1)S(1)} collective-permute-done((bf16[1024,512]{1,0:T(8,128)(2,1)S(1)}, bf16[1024,512]{1,0:T(8,128)(2,1)S(1)}, u32[]{:S(2)}, u32[]{:S(2)}) %collective-permute-start.46) | collective-permute-done | bytes 1048608 | tf_op jit(solution)/shard_map/ppermute | solution.py:345
  154.3 10.6 %attention.5.refs_0_ = bf16[1536,256]{1,0:T(8,128)(2,1)} custom-call(s32[3]{0:T(128)} %pad_add_fusion.place, bf16[384,256]{1,0:T(8,128)(2,1)} %get-tuple-element.51.refs_0_, bf16[384,256]{1,0:T(8,128)(2,1)} %copy-done.50, bf16[384,256]{1,0:T(8,128)(2,1)} %copy-done.56, bf16[384,256]{1,0:T(8,128)(2,1)} %copy-done.57, bf16[384,256]{1,0:T(8,128)(2,1)} %refs_4_.5, ...), custom_call_target="tpu_custom_call" | custom-call | flops 14495514624 | bytes 6291456 | tf_op jit(solution)/shard_map/attention/pallas_call | solution.py:186
  165.8 5.7 %collective-permute-done.31.refs_5_.refs_13_ = bf16[1536,128]{1,0:T(8,128)(2,1)S(1)} collective-permute-done((bf16[1536,128]{1,0:T(8,128)(2,1)}, bf16[1536,128]{1,0:T(8,128)(2,1)S(1)}, u32[]{:S(2)}, u32[]{:S(2)}) %collective-permute-start.31) | collective-permute-done | bytes 393248 | tf_op jit(solution)/shard_map/ppermute | solution.py:329
  172.1 7.8 %collective-permute-start.66 = (bf16[1024,384]{1,0:T(8,128)(2,1)S(1)}, bf16[1024,384]{1,0:T(8,128)(2,1)S(1)}, u32[]{:S(2)}, u32[]{:S(2)}) collective-permute-start(bf16[1024,384]{1,0:T(8,128)(2,1)S(1)} %constant_dynamic-update-slice_fusion.7.refs_24_), channel_id=1, source_target_pairs={{0,16},{8,24},{16,0},{24,8},{1,17},{9,25},{17,1},{25,9},{2,18},{10... | collective-permute-start | bytes 2359304 | tf_op jit(solution)/shard_map/ppermute | solution.py:345
  181.5 9.5 %collective-permute-start.65 = (bf16[1024,384]{1,0:T(8,128)(2,1)S(1)}, bf16[1024,384]{1,0:T(8,128)(2,1)S(1)}, u32[]{:S(2)}, u32[]{:S(2)}) collective-permute-start(bf16[1024,384]{1,0:T(8,128)(2,1)S(1)} %constant_dynamic-update-slice_fusion.7.refs_24_), channel_id=1, source_target_pairs={{0,8},{8,0},{16,24},{24,16},{1,9},{9,1},{17,25},{25,17},{2,10},{10... | collective-permute-start | bytes 2359304 | tf_op jit(solution)/shard_map/ppermute | solution.py:345
  194.7 20.5 %collective-permute-done.66.refs_26_ = bf16[1024,384]{1,0:T(8,128)(2,1)S(1)} collective-permute-done((bf16[1024,384]{1,0:T(8,128)(2,1)S(1)}, bf16[1024,384]{1,0:T(8,128)(2,1)S(1)}, u32[]{:S(2)}, u32[]{:S(2)}) %collective-permute-start.66) | collective-permute-done | bytes 786464 | tf_op jit(solution)/shard_map/ppermute | solution.py:345
  218.3 9.9 %collective-permute-done.53.refs_2_ = bf16[1536,256]{1,0:T(8,128)(2,1)} collective-permute-done((bf16[1536,256]{1,0:T(8,128)(2,1)}, bf16[1536,256]{1,0:T(8,128)(2,1)}, u32[]{:S(2)}, u32[]{:S(2)}) %collective-permute-start.53) | collective-permute-done | bytes 786464 | tf_op jit(solution)/shard_map/ppermute | solution.py:329
  228.2 6.0 %collective-permute-done.52.refs_1_ = bf16[1536,256]{1,0:T(8,128)(2,1)} collective-permute-done((bf16[1536,256]{1,0:T(8,128)(2,1)}, bf16[1536,256]{1,0:T(8,128)(2,1)}, u32[]{:S(2)}, u32[]{:S(2)}) %collective-permute-start.52) | collective-permute-done | bytes 786464 | tf_op jit(solution)/shard_map/ppermute | solution.py:329
  235.0 16.9 %collective-permute-done.68.refs_28_ = bf16[1024,384]{1,0:T(8,128)(2,1)S(1)} collective-permute-done((bf16[1024,384]{1,0:T(8,128)(2,1)S(1)}, bf16[1024,384]{1,0:T(8,128)(2,1)S(1)}, u32[]{:S(2)}, u32[]{:S(2)}) %collective-permute-start.68) | collective-permute-done | bytes 786464 | tf_op jit(solution)/shard_map/ppermute | solution.py:345
  257.1 14.6 %project.5 = (bf16[384,384]{1,0:T(8,128)(2,1)}, bf16[384,384]{1,0:T(8,128)(2,1)}, bf16[384,384]{1,0:T(8,128)(2,1)}, bf16[384,384]{1,0:T(8,128)(2,1)}) custom-call(s32[6]{0:T(128)} %stack.115.scalars, bf16[1536,256]{1,0:T(8,128)(2,1)} %attention.5.refs_0_, bf16[1536,256]{1,0:T(8,128)(2,1)} %collective-permute-done.52.refs_1_, ...), custom_call_target="tpu_custom_call" | custom-call | flops 4831838208 | bytes 15728640 | tf_op jit(solution)/shard_map/project/pallas_call | solution.py:280
  278.0 21.4 %collective-permute-done.51.refs_12_.refs_20_ = bf16[1024,512]{1,0:T(8,128)(2,1)} collective-permute-done((bf16[1024,512]{1,0:T(8,128)(2,1)S(1)}, bf16[1024,512]{1,0:T(8,128)(2,1)}, u32[]{:S(2)}, u32[]{:S(2)}) %collective-permute-start.51) | collective-permute-done | bytes 1048608 | tf_op jit(solution)/shard_map/ppermute | solution.py:345
  299.4 9.5 %project.3.refs_21_ = f32[1536,512]{1,0:T(8,128)} custom-call(s32[4]{0:T(128)} %add_add_fusion.1.scalars, bf16[1536,256]{1,0:T(8,128)(2,1)} %attention.5.refs_0_, bf16[1536,256]{1,0:T(8,128)(2,1)} %collective-permute-done.52.refs_1_, bf16[1536,256]{1,0:T(8,128)(2,1)} %collective-permute-done.53.refs_2_, bf16[1536,256]{1,0:T(8,128)(2,1)} %copy-done.3, ...), custom_call_target="tpu_custom_call" | custom-call | flops 3221225472 | bytes 8388608 | tf_op jit(solution)/shard_map/project/pallas_call | solution.py:280
  308.9 10.8 %project.4 = (bf16[384,512]{1,0:T(8,128)(2,1)}, bf16[384,512]{1,0:T(8,128)(2,1)}, bf16[384,512]{1,0:T(8,128)(2,1)}, bf16[384,512]{1,0:T(8,128)(2,1)}) custom-call(s32[4]{0:T(128)} %add_add_fusion.scalars, bf16[1536,128]{1,0:T(8,128)(2,1)} %attention.3.refs_0_.refs_8_, bf16[1536,128]{1,0:T(8,128)(2,1)} %attention.4.refs_1_.refs_9_, ...), custom_call_target="tpu_custom_call" | custom-call | flops 3221225472 | bytes 8388608 | tf_op jit(solution)/shard_map/project/pallas_call | solution.py:280
  324.6 7.5 %collective-permute-done.59 = bf16[384,512]{1,0:T(8,128)(2,1)S(1)} collective-permute-done((bf16[384,512]{1,0:T(8,128)(2,1)}, bf16[384,512]{1,0:T(8,128)(2,1)S(1)}, u32[]{:S(2)}, u32[]{:S(2)}) %collective-permute-start.59) | collective-permute-done | bytes 393248 | tf_op jit(solution)/shard_map/ppermute | solution.py:329
  332.1 6.8 %collective-permute-done.61 = bf16[384,512]{1,0:T(8,128)(2,1)S(1)} collective-permute-done((bf16[384,512]{1,0:T(8,128)(2,1)}, bf16[384,512]{1,0:T(8,128)(2,1)S(1)}, u32[]{:S(2)}, u32[]{:S(2)}) %collective-permute-start.61) | collective-permute-done | bytes 393248 | tf_op jit(solution)/shard_map/ppermute | solution.py:329
  (271 shorter events, 93.7 us)
Async XLA Ops:
  0.0 22.8 %collective-permute-start.10 = (bf16[384,256]{1,0:T(8,128)(2,1)}, bf16[384,256]{1,0:T(8,128)(2,1)S(1)}, u32[]{:S(2)}, u32[]{:S(2)}) collective-permute-start(bf16[384,256]{1,0:T(8,128)(2,1)} %refs_4_.5), channel_id=1, source_target_pairs={{0,24},{1,25},{2,26},{3,27},{4,28},{5,29},{6,30},{7,31}} | collective-permute-start | bytes 589832 | tf_op jit(solution)/shard_map/ppermute | solution.py:338
  34.4 45.8 %collective-permute-start.14 = (bf16[1152,256]{1,0:T(8,128)(2,1)S(1)}, bf16[1152,256]{1,0:T(8,128)(2,1)S(1)}, u32[]{:S(2)}, u32[]{:S(2)}) collective-permute-start(bf16[1152,256]{1,0:T(8,128)(2,1)S(1)} %constant_dynamic-update-slice_fusion.refs_12_), channel_id=1, source_target_pairs={{0,4},{2,6},{4,0},{6,2},{1,5},{3,7},{5,1},{7,3},{8,12},{10,14},{12... | collective-permute-start | bytes 1769480 | tf_op jit(solution)/shard_map/ppermute | solution.py:329
  37.5 43.2 %collective-permute-start.13 = (bf16[1152,256]{1,0:T(8,128)(2,1)S(1)}, bf16[1152,256]{1,0:T(8,128)(2,1)S(1)}, u32[]{:S(2)}, u32[]{:S(2)}) collective-permute-start(bf16[1152,256]{1,0:T(8,128)(2,1)S(1)} %constant_dynamic-update-slice_fusion.refs_12_), channel_id=1, source_target_pairs={{0,2},{2,0},{4,6},{6,4},{1,3},{3,1},{5,7},{7,5},{8,10},{10,8},{12,... | collective-permute-start | bytes 1769480 | tf_op jit(solution)/shard_map/ppermute | solution.py:329
  44.7 24.5 %collective-permute-start.42 = (bf16[256,512]{1,0:T(8,128)(2,1)}, bf16[256,512]{1,0:T(8,128)(2,1)S(1)}, u32[]{:S(2)}, u32[]{:S(2)}) collective-permute-start(bf16[256,512]{1,0:T(8,128)(2,1)} %get-tuple-element.48), channel_id=1, source_target_pairs={{0,2},{2,0},{4,6},{6,4},{1,3},{3,1},{5,7},{7,5},{8,10},{10,8},{12,... | collective-permute-start | bytes 786440 | tf_op jit(solution)/shard_map/ppermute | solution.py:329
  102.8 47.8 %collective-permute-start.46 = (bf16[1024,512]{1,0:T(8,128)(2,1)S(1)}, bf16[1024,512]{1,0:T(8,128)(2,1)S(1)}, u32[]{:S(2)}, u32[]{:S(2)}) collective-permute-start(bf16[1024,512]{1,0:T(8,128)(2,1)S(1)} %constant_dynamic-update-slice_fusion.3.refs_8_.refs_16_), channel_id=1, source_target_pairs={{0,16},{8,24},{16,0},{24,8},{1,17},{9,25},{17,1},{25,9},{2,18},{10... | collective-permute-start | bytes 3145736 | tf_op jit(solution)/shard_map/ppermute | solution.py:345
  111.7 38.9 %collective-permute-start.34 = (bf16[1536,128]{1,0:T(8,128)(2,1)}, bf16[1536,128]{1,0:T(8,128)(2,1)S(1)}, u32[]{:S(2)}, u32[]{:S(2)}) collective-permute-start(bf16[1536,128]{1,0:T(8,128)(2,1)} %attention.3.refs_0_.refs_8_), channel_id=1, source_target_pairs={{1,0},{0,1},{3,2},{2,3},{5,4},{4,5},{7,6},{6,7},{9,8},{8,9},{11,10... | collective-permute-start | bytes 1179656 | tf_op jit(solution)/shard_map/ppermute | solution.py:341
  111.8 39.8 %collective-permute-start.32 = (bf16[1536,128]{1,0:T(8,128)(2,1)}, bf16[1536,128]{1,0:T(8,128)(2,1)S(1)}, u32[]{:S(2)}, u32[]{:S(2)}) collective-permute-start(bf16[1536,128]{1,0:T(8,128)(2,1)} %attention.3.refs_0_.refs_8_), channel_id=1, source_target_pairs={{0,6},{2,4},{4,2},{6,0},{1,7},{3,5},{5,3},{7,1},{8,14},{10,12},{12... | collective-permute-start | bytes 1179656 | tf_op jit(solution)/shard_map/ppermute | solution.py:329
  113.8 38.9 %collective-permute-start.30 = (bf16[1536,128]{1,0:T(8,128)(2,1)}, bf16[1536,128]{1,0:T(8,128)(2,1)S(1)}, u32[]{:S(2)}, u32[]{:S(2)}) collective-permute-start(bf16[1536,128]{1,0:T(8,128)(2,1)} %attention.3.refs_0_.refs_8_), channel_id=1, source_target_pairs={{0,4},{2,6},{4,0},{6,2},{1,5},{3,7},{5,1},{7,3},{8,12},{10,14},{12... | collective-permute-start | bytes 1179656 | tf_op jit(solution)/shard_map/ppermute | solution.py:329
  121.7 43.2 %collective-permute-start.28 = (bf16[1536,128]{1,0:T(8,128)(2,1)S(1)}, bf16[1536,128]{1,0:T(8,128)(2,1)S(1)}, u32[]{:S(2)}, u32[]{:S(2)}) collective-permute-start(bf16[1536,128]{1,0:T(8,128)(2,1)S(1)} %copy-done.7), channel_id=1, source_target_pairs={{0,2},{2,0},{4,6},{6,4},{1,3},{3,1},{5,7},{7,5},{8,10},{10,8},{12,... | collective-permute-start | bytes 1179656 | tf_op jit(solution)/shard_map/ppermute | solution.py:329
  172.1 43.1 %collective-permute-start.66 = (bf16[1024,384]{1,0:T(8,128)(2,1)S(1)}, bf16[1024,384]{1,0:T(8,128)(2,1)S(1)}, u32[]{:S(2)}, u32[]{:S(2)}) collective-permute-start(bf16[1024,384]{1,0:T(8,128)(2,1)S(1)} %constant_dynamic-update-slice_fusion.7.refs_24_), channel_id=1, source_target_pairs={{0,16},{8,24},{16,0},{24,8},{1,17},{9,25},{17,1},{25,9},{2,18},{10... | collective-permute-start | bytes 2359304 | tf_op jit(solution)/shard_map/ppermute | solution.py:345
  179.9 35.8 %collective-permute-start.67 = (bf16[1024,384]{1,0:T(8,128)(2,1)S(1)}, bf16[1024,384]{1,0:T(8,128)(2,1)}, u32[]{:S(2)}, u32[]{:S(2)}) collective-permute-start(bf16[1024,384]{1,0:T(8,128)(2,1)S(1)} %constant_dynamic-update-slice_fusion.7.refs_24_), channel_id=1, source_target_pairs={{8,16},{16,8},{9,17},{17,9},{10,18},{18,10},{11,19},{19,11},{12,20... | collective-permute-start | bytes 2359304 | tf_op jit(solution)/shard_map/ppermute | solution.py:345
  181.5 35.4 %collective-permute-start.65 = (bf16[1024,384]{1,0:T(8,128)(2,1)S(1)}, bf16[1024,384]{1,0:T(8,128)(2,1)S(1)}, u32[]{:S(2)}, u32[]{:S(2)}) collective-permute-start(bf16[1024,384]{1,0:T(8,128)(2,1)S(1)} %constant_dynamic-update-slice_fusion.7.refs_24_), channel_id=1, source_target_pairs={{0,8},{8,0},{16,24},{24,16},{1,9},{9,1},{17,25},{25,17},{2,10},{10... | collective-permute-start | bytes 2359304 | tf_op jit(solution)/shard_map/ppermute | solution.py:345
  191.0 27.2 %collective-permute-start.54 = (bf16[1536,256]{1,0:T(8,128)(2,1)}, bf16[1536,256]{1,0:T(8,128)(2,1)S(1)}, u32[]{:S(2)}, u32[]{:S(2)}) collective-permute-start(bf16[1536,256]{1,0:T(8,128)(2,1)} %attention.5.refs_0_), channel_id=1, source_target_pairs={{0,6},{2,4},{4,2},{6,0},{1,7},{3,5},{5,3},{7,1},{8,14},{10,12},{12... | collective-permute-start | bytes 2359304 | tf_op jit(solution)/shard_map/ppermute | solution.py:329
  193.6 34.6 %collective-permute-start.53 = (bf16[1536,256]{1,0:T(8,128)(2,1)}, bf16[1536,256]{1,0:T(8,128)(2,1)}, u32[]{:S(2)}, u32[]{:S(2)}) collective-permute-start(bf16[1536,256]{1,0:T(8,128)(2,1)} %attention.5.refs_0_), channel_id=1, source_target_pairs={{0,4},{2,6},{4,0},{6,2},{1,5},{3,7},{5,1},{7,3},{8,12},{10,14},{12... | collective-permute-start | bytes 2359304 | tf_op jit(solution)/shard_map/ppermute | solution.py:329
  216.9 34.9 %collective-permute-start.68 = (bf16[1024,384]{1,0:T(8,128)(2,1)S(1)}, bf16[1024,384]{1,0:T(8,128)(2,1)S(1)}, u32[]{:S(2)}, u32[]{:S(2)}) collective-permute-start(bf16[1024,384]{1,0:T(8,128)(2,1)S(1)} %collective-permute-done.66.refs_26_), channel_id=1, source_target_pairs={{8,0},{16,24},{9,1},{17,25},{10,2},{18,26},{11,3},{19,27},{12,4},{... | collective-permute-start | bytes 2359304 | tf_op jit(solution)/shard_map/ppermute | solution.py:345
  218.2 33.6 %collective-permute-start.58 = (bf16[1536,256]{1,0:T(8,128)(2,1)S(1)}, bf16[1536,256]{1,0:T(8,128)(2,1)S(1)}, u32[]{:S(2)}, u32[]{:S(2)}) collective-permute-start(bf16[1536,256]{1,0:T(8,128)(2,1)S(1)} %collective-permute-done.54.refs_3_), channel_id=1, source_target_pairs={{1,0},{0,1},{3,2},{2,3},{5,4},{4,5},{7,6},{6,7},{9,8},{8,9},{11,10... | collective-permute-start | bytes 2359304 | tf_op jit(solution)/shard_map/ppermute | solution.py:341
  228.2 28.9 %collective-permute-start.57 = (bf16[1536,256]{1,0:T(8,128)(2,1)}, bf16[1536,256]{1,0:T(8,128)(2,1)}, u32[]{:S(2)}, u32[]{:S(2)}) collective-permute-start(bf16[1536,256]{1,0:T(8,128)(2,1)} %collective-permute-done.53.refs_2_), channel_id=1, source_target_pairs={{1,0},{0,1},{3,2},{2,3},{5,4},{4,5},{7,6},{6,7},{9,8},{8,9},{11,10... | collective-permute-start | bytes 2359304 | tf_op jit(solution)/shard_map/ppermute | solution.py:341
  234.2 22.9 %collective-permute-start.56 = (bf16[1536,256]{1,0:T(8,128)(2,1)}, bf16[1536,256]{1,0:T(8,128)(2,1)}, u32[]{:S(2)}, u32[]{:S(2)}) collective-permute-start(bf16[1536,256]{1,0:T(8,128)(2,1)} %collective-permute-done.52.refs_1_), channel_id=1, source_target_pairs={{1,0},{0,1},{3,2},{2,3},{5,4},{4,5},{7,6},{6,7},{9,8},{8,9},{11,10... | collective-permute-start | bytes 2359304 | tf_op jit(solution)/shard_map/ppermute | solution.py:341
  234.2 39.0 %collective-permute-start.47 = (bf16[1024,512]{1,0:T(8,128)(2,1)S(1)}, bf16[1024,512]{1,0:T(8,128)(2,1)S(1)}, u32[]{:S(2)}, u32[]{:S(2)}) collective-permute-start(bf16[1024,512]{1,0:T(8,128)(2,1)S(1)} %constant_dynamic-update-slice_fusion.3.refs_8_.refs_16_), channel_id=1, source_target_pairs={{8,16},{16,8},{9,17},{17,9},{10,18},{18,10},{11,19},{19,11},{12,20... | collective-permute-start | bytes 3145736 | tf_op jit(solution)/shard_map/ppermute | solution.py:345
  251.8 26.1 %collective-permute-start.45 = (bf16[1024,512]{1,0:T(8,128)(2,1)S(1)}, bf16[1024,512]{1,0:T(8,128)(2,1)}, u32[]{:S(2)}, u32[]{:S(2)}) collective-permute-start(bf16[1024,512]{1,0:T(8,128)(2,1)S(1)} %constant_dynamic-update-slice_fusion.3.refs_8_.refs_16_), channel_id=1, source_target_pairs={{0,8},{8,0},{16,24},{24,16},{1,9},{9,1},{17,25},{25,17},{2,10},{10... | collective-permute-start | bytes 3145736 | tf_op jit(solution)/shard_map/ppermute | solution.py:345
  253.6 45.7 %collective-permute-start.51 = (bf16[1024,512]{1,0:T(8,128)(2,1)S(1)}, bf16[1024,512]{1,0:T(8,128)(2,1)}, u32[]{:S(2)}, u32[]{:S(2)}) collective-permute-start(bf16[1024,512]{1,0:T(8,128)(2,1)S(1)} %collective-permute-done.46.refs_10_.refs_18_), channel_id=1, source_target_pairs={{8,0},{16,24},{9,1},{17,25},{10,2},{18,26},{11,3},{19,27},{12,4},{... | collective-permute-start | bytes 3145736 | tf_op jit(solution)/shard_map/ppermute | solution.py:345
  271.7 49.5 %collective-permute-start.69 = (bf16[384,384]{1,0:T(8,128)(2,1)}, bf16[384,384]{1,0:T(8,128)(2,1)S(1)}, u32[]{:S(2)}, u32[]{:S(2)}) collective-permute-start(bf16[384,384]{1,0:T(8,128)(2,1)} %get-tuple-element.70), channel_id=1, source_target_pairs={{0,2},{2,0},{4,6},{6,4},{1,3},{3,1},{5,7},{7,5},{8,10},{10,8},{12,... | collective-permute-start | bytes 884744 | tf_op jit(solution)/shard_map/ppermute | solution.py:329
  272.3 51.0 %collective-permute-start.70 = (bf16[384,384]{1,0:T(8,128)(2,1)}, bf16[384,384]{1,0:T(8,128)(2,1)}, u32[]{:S(2)}, u32[]{:S(2)}) collective-permute-start(bf16[384,384]{1,0:T(8,128)(2,1)} %get-tuple-element.71), channel_id=1, source_target_pairs={{0,4},{2,6},{4,0},{6,2},{1,5},{3,7},{5,1},{7,3},{8,12},{10,14},{12... | collective-permute-start | bytes 884744 | tf_op jit(solution)/shard_map/ppermute | solution.py:329
  273.2 50.1 %collective-permute-start.71 = (bf16[384,384]{1,0:T(8,128)(2,1)}, bf16[384,384]{1,0:T(8,128)(2,1)}, u32[]{:S(2)}, u32[]{:S(2)}) collective-permute-start(bf16[384,384]{1,0:T(8,128)(2,1)} %get-tuple-element.72), channel_id=1, source_target_pairs={{0,6},{2,4},{4,2},{6,0},{1,7},{3,5},{5,3},{7,1},{8,14},{10,12},{12... | collective-permute-start | bytes 884744 | tf_op jit(solution)/shard_map/ppermute | solution.py:329
  (106 other events, 2537.0 us)
